TPU v7x, 128 devices: a whole 4x4x4 slice. The times are simulated.
128 devices in a mesh: face: 4 (over z_lo, core), tile: 32 (over z_hi, x, y).
Axes of the slice: x: 4, y: 4, z: 4 (z_hi: 2, z_lo: 2; z = z_hi * 2 + z_lo), core: 2. Of those that a mesh axis runs over, the one named last changes fastest.
Arguments:
- atmos_state: bfloat16 [32, 12, 256, 256], P(None, 'face', 'tile'), may hold values from -6 to 6
- land_sea: int32 [12, 256, 256], P('face', 'tile'), may hold values 0 or 1
- owners: int32 [3072, 1], P(('face', 'tile')), may hold values from 0 to 31; in each aligned block of 24 rows (0 to 23, 24 to 47, ...) at most 2 rows name the same one
- seam_table: int32 [48, 2], replicated, may hold values from 0 to 47, as said below
- ocean_state: float32 [4, 32, 64, 2, 256], P('face', 'tile'), may hold values from -6 to 6
- conv_input: bfloat16 [3, 64, 96], replicated, may hold values from -0.375 to 0.375
- conv_encode: bfloat16 [3, 64, 192], replicated, may hold values from -0.25 to 0.25
- conv_coarse: bfloat16 [3, 64, 192], replicated, may hold values from -0.25 to 0.25
- conv_decode: bfloat16 [3, 64, 384], replicated, may hold values from -0.1875 to 0.1875
- output_head: bfloat16 [12, 64], replicated, may hold values from -0.75 to 0.75
- ocean_in: float32 [64, 6], replicated, may hold values from -2.5 to 2.5
- ocean_out: float32 [64], replicated, may hold values from -0.75 to 0.75
Outputs:
- atmos_next: bfloat16 [8, 12, 256, 256], P(None, 'face', 'tile')
- ocean_next: float32 [4, 32, 64, 2, 256], P('face', 'tile')
Inputs may be any that keep to these rules, and one draw needn't show every extreme that they name: `owners`: among the 24 tiles of one face group and stripe (an aligned block of rows) no owner appears more than 2 times, and that bound is reached in some block. `seam_table`: row 4 g + s describes side s of face g. Column 0 names the partner side 4 h + u; the pairing is an involution with no fixed points, and paired sides carry the same reversal flag in column 1 (0 or 1).
All inputs are finite; a program needn't handle non-finite values. No bound on the sum of `land_sea` on one device may be relied on, other than what follows from the above.
Results may differ from a plain program's by a relative error of at most 0.0028.
Values may be sent and summed in bfloat16 or wider, within the bound.
A program may use at most 64 MiB of HBM per device.

v0:
```python
import jax
import jax.numpy as jnp
from jax import lax
from jax.sharding import PartitionSpec as P

OUT_VARS = 8
FLUX_CH = 4
OCEAN_CH = 2


def extended(shard, sides, width):
    for axis, dim in sides:
        size, length = (lax.axis_size(axis), shard.shape[dim])
        up = [(i, (i + 1) % size) for i in range(size)]
        down = [(j, i) for i, j in up]
        last = lax.slice_in_dim(shard, length - width, length, axis=dim)
        initial = lax.slice_in_dim(shard, 0, width, axis=dim)
        before = lax.ppermute(last, axis, up)
        after = lax.ppermute(initial, axis, down)
        shard = jnp.concatenate([before, shard, after], axis=dim)
    return shard


def sent_to_all(shard, axis):
    copies = jnp.broadcast_to(shard, (lax.axis_size(axis), *shard.shape))
    return lax.all_to_all(copies, axis, split_axis=0, concat_axis=0, tiled=True)


def joined_along(tiles, dim):
    dims = list(tiles.shape[1:])
    dims[dim] *= tiles.shape[0]
    return jnp.moveaxis(tiles, 0, dim).reshape(dims)


def collect(shard, axis, dim):
    tiles = sent_to_all(shard, axis)
    return joined_along(tiles, dim)


def pad_field(values, seam_table):
    channels, faces_dev, stripe_rows, face_side = values.shape
    tile_count = lax.axis_size("tile")
    stripe = lax.axis_index("tile")
    face_group = lax.axis_index("face")
    rimmed = extended(values, (("tile", 2),), 1)
    edge_rows = jnp.stack([values[:, :, 0, :], rimmed[:, :, 0, :]], axis=2)
    edge_pieces = edge_rows.reshape(channels, faces_dev, 2, tile_count, stripe_rows)
    received = lax.all_to_all(edge_pieces, "tile", split_axis=3, concat_axis=3, tiled=True)
    row_part = received[:, :, :, 0, :]
    row_start = stripe * stripe_rows
    col_part = jnp.stack([values[:, :, :, 0], values[:, :, :, face_side - 1]], axis=2)
    seam_piece = jnp.concatenate([row_part, col_part], axis=2)
    seam_piece = jnp.transpose(seam_piece, (1, 2, 0, 3)).reshape(
        1, faces_dev, 4, channels * stripe_rows
    )
    own_sides = lax.dynamic_slice_in_dim(seam_table, face_group * (faces_dev * 4), faces_dev * 4, 0)
    grouped = lax.all_gather(seam_piece, "face", axis=0, tiled=True)
    piece_table = grouped.reshape(grouped.shape[0] * faces_dev * 4, channels * stripe_rows)
    picked = jnp.take(piece_table, own_sides[:, 0], axis=0)
    collected = collect(picked[None], "tile", 0)
    collected = collected.reshape(tile_count, faces_dev * 4, channels, stripe_rows)
    strips = jnp.transpose(collected, (1, 2, 0, 3)).reshape(faces_dev * 4, channels, face_side)
    strips = jnp.where(own_sides[:, 1][:, None, None] == 1, strips[:, :, ::-1], strips)
    strips = jnp.transpose(strips.reshape(faces_dev, 4, channels, face_side), (2, 0, 1, 3))
    upper_row = jnp.where(stripe == 0, strips[:, :, 0, :], rimmed[:, :, 0, :])
    bottom = jnp.where(
        stripe == tile_count - 1, strips[:, :, 1, :], rimmed[:, :, stripe_rows + 1, :]
    )
    middle = jnp.concatenate([upper_row[:, :, None, :], values, bottom[:, :, None, :]], axis=2)
    zero_cells = jnp.zeros((channels, faces_dev, 2, 1), values.dtype)
    columns = jnp.concatenate([zero_cells, strips[:, :, 2:, :], zero_cells], axis=3)
    columns = lax.dynamic_slice_in_dim(columns, row_start, stripe_rows + 2, 3)
    return jnp.concatenate([columns[:, :, 0, :, None], middle, columns[:, :, 1, :, None]], axis=3)


def convolve(padded, weight):
    channels, faces_dev, rows_two, side_two = padded.shape
    stripe_rows = rows_two - 2
    face_side = side_two - 2
    planes = []
    for face_index in range(faces_dev):
        summed = jnp.zeros((weight.shape[1], stripe_rows * face_side), jnp.float32)
        for row_shift in range(3):
            tap_rows = jnp.concatenate(
                [
                    padded[
                        :,
                        face_index,
                        row_shift : row_shift + stripe_rows,
                        col_shift : col_shift + face_side,
                    ]
                    for col_shift in range(3)
                ],
                axis=0,
            )
            summed = summed + jnp.dot(
                weight[row_shift],
                tap_rows.reshape(3 * channels, stripe_rows * face_side),
                preferred_element_type=jnp.float32,
            )
        planes.append(jax.nn.gelu(summed).astype(jnp.bfloat16).reshape(-1, stripe_rows, face_side))
    return jnp.stack(planes, axis=1)


def upsample(values):
    return jnp.repeat(jnp.repeat(values, 2, axis=2), 2, axis=3)


def ocean_update(held_state, arrived_flux, ocean_in, ocean_out):
    stacked = jnp.concatenate([held_state, arrived_flux.astype(jnp.float32)], axis=1)
    hidden = jax.nn.gelu(
        jnp.einsum("hc,ncs->nhs", ocean_in, stacked, precision=lax.Precision.HIGHEST)
    )
    sea_now = held_state[:, 0] + jnp.einsum(
        "h,nhs->ns", ocean_out, hidden, precision=lax.Precision.HIGHEST
    )
    return jnp.stack([sea_now, held_state[:, 0]], axis=1)


def ocean_blocks(held_state, arrived_flux, ocean_in, ocean_out, block_count):
    slot_count, state_ch, face_side = held_state.shape
    capacity = slot_count // block_count
    held_split = held_state.reshape(block_count, capacity, state_ch, face_side)
    flux_split = arrived_flux.reshape(block_count, capacity, arrived_flux.shape[1], face_side)
    stepped = lax.map(
        lambda pair: ocean_update(pair[0], pair[1], ocean_in, ocean_out), (held_split, flux_split)
    )
    return stepped.reshape(slot_count, state_ch, face_side)


def on_device(
    atmos_state,
    land_sea,
    owners,
    seam_table,
    ocean_state,
    conv_input,
    conv_encode,
    conv_coarse,
    conv_decode,
    output_head,
    ocean_in,
    ocean_out,
):
    encoded = convolve(pad_field(atmos_state, seam_table), conv_input)
    skip_level = convolve(pad_field(encoded, seam_table), conv_encode)
    channels, faces_dev, stripe_rows, face_side = skip_level.shape
    pooled = (
        skip_level.astype(jnp.float32)
        .reshape(channels, faces_dev, stripe_rows // 2, 2, face_side // 2, 2)
        .mean(axis=(3, 5))
        .astype(jnp.bfloat16)
    )
    coarse_out = convolve(pad_field(pooled, seam_table), conv_coarse)
    coarse_pad = upsample(pad_field(coarse_out, seam_table))[
        :, :, 1 : stripe_rows + 3, 1 : face_side + 3
    ]
    padded = jnp.concatenate([pad_field(skip_level, seam_table), coarse_pad], axis=0)
    decoded = convolve(padded, conv_decode)
    head_out = jnp.dot(
        output_head, decoded.reshape(channels, -1), preferred_element_type=jnp.float32
    )
    head_out = head_out.reshape(-1, faces_dev, stripe_rows, face_side)
    predicted = atmos_state[:OUT_VARS].astype(jnp.float32) + head_out[:OUT_VARS]
    is_ocean = land_sea == 1
    fluxes = jnp.where(is_ocean[None], head_out[OUT_VARS:], 0.0).astype(jnp.bfloat16)
    flux_tiles = jnp.transpose(fluxes, (1, 2, 0, 3)).reshape(
        faces_dev * stripe_rows, FLUX_CH * face_side
    )
    tile_count = lax.axis_size("tile")
    owner_ids = owners[:, 0]
    owner_hits = (owner_ids[:, None] == jnp.arange(tile_count)[None, :]).astype(jnp.int32)
    slot_rank = jnp.sum((jnp.cumsum(owner_hits, axis=0) - 1) * owner_hits, axis=1)
    slot_count = ocean_state.shape[2]
    capacity = slot_count // tile_count
    slot_index = owner_ids * capacity + slot_rank
    selector = (jnp.arange(slot_count)[:, None] == slot_index[None, :]).astype(jnp.bfloat16)
    outgoing = jnp.dot(selector, flux_tiles, preferred_element_type=jnp.float32).astype(
        jnp.bfloat16
    )
    outgoing = outgoing.reshape(tile_count, capacity, FLUX_CH, face_side)
    held_state = ocean_state[0, 0]
    visiting = lax.all_to_all(
        held_state.reshape(tile_count, capacity, OCEAN_CH, face_side),
        "tile",
        split_axis=0,
        concat_axis=0,
        tiled=True,
    )
    stepped = ocean_blocks(
        visiting.reshape(slot_count, OCEAN_CH, face_side),
        outgoing.reshape(slot_count, FLUX_CH, face_side),
        ocean_in,
        ocean_out,
        tile_count,
    )
    sea_slots = stepped[:, 0].astype(jnp.bfloat16)
    renewed = lax.all_to_all(
        stepped.reshape(tile_count, capacity, OCEAN_CH, face_side),
        "tile",
        split_axis=0,
        concat_axis=0,
        tiled=True,
    )
    renewed = renewed.reshape(slot_count, OCEAN_CH, face_side)
    sea_tiles = jnp.dot(selector.T, sea_slots, preferred_element_type=jnp.float32)
    sea_temp = sea_tiles.reshape(faces_dev, stripe_rows, face_side)
    surface = jnp.where(is_ocean, sea_temp, predicted[0])
    atmos_next = jnp.concatenate([surface[None], predicted[1:]], axis=0).astype(jnp.bfloat16)
    return (atmos_next, renewed.reshape(1, 1, slot_count, OCEAN_CH, face_side))


def solution(mesh):
    in_specs = (
        P(None, "face", "tile", None),
        P("face", "tile", None),
        P(("face", "tile"), None),
        P(),
        P("face", "tile", None, None, None),
        P(),
        P(),
        P(),
        P(),
        P(),
        P(),
        P(),
    )
    out_specs = (P(None, "face", "tile", None), P("face", "tile", None, None, None))
    return jax.shard_map(
        on_device, mesh=mesh, in_specs=in_specs, out_specs=out_specs, check_vma=False
    )
```

profile of v0, /device:TPU:1, one launch (start us, length us, event | category | flops | bytes accessed | tf_op | source)
XLA Modules:
  0.0 460.2 jit_solution(17846678149532458649)
XLA Ops:
  4.8 7.0 %collective-permute-start.1 = (bf16[32,3,1,256]{3,0,2,1:T(8,128)(2,1)}, bf16[32,3,1,256]{3,0,2,1:T(8,128)(2,1)}, u32[]{:S(2)}, u32[]{:S(2)}) collective-permute-start(bf16[32,3,1,256]{3,0,2,1:T(8,128)(2,1)} %copy.591), channel_id=1, source_target_pairs={{1,0},{2,1},{3,2},{4,3},{5,4},{6,5},{7,6},{8,7},{9,8},{10,9},{11,1... | collective-permute-start | bytes 147464 | tf_op jit(solution)/shard_map/ppermute | solution.py:19
  16.3 4.2 all-to-all-start.1
  20.6 8.7 %all-to-all-done.1 = bf16[32,2,768]{2,1,0:T(2,128)(2,1)S(1)} async-done(((bf16[32,2,768]{2,1,0:T(2,128)(2,1)}), bf16[32,2,768]{2,1,0:T(2,128)(2,1)S(1)}, u32[]{:S(2)}, u32[]{:S(2)}) %all-to-all-start.1) | async-done | bytes 98336 | tf_op jit(solution)/shard_map/all_to_all | solution.py:48
  29.8 7.7 %all_gather.15 = bf16[4,3,4,256]{3,2,1,0:T(4,128)(2,1)S(1)} all-gather(bf16[1,3,4,256]{3,2,1,0:T(4,128)(2,1)S(1)} %reshape.415), channel_id=1, replica_groups=mesh['face'=4,'tile'=32] {'face'}, dimensions={0}, use_global_device_ids=true | all-gather | bytes 30720 | tf_op jit(solution)/shard_map/all_gather | solution.py:57
  43.0 9.9 %all-to-all-done.2 = bf16[32,1,12,256]{3,2,1,0:T(8,128)(2,1)S(1)} async-done(((bf16[32,1,12,256]{3,2,1,0:T(8,128)(2,1)}), bf16[32,1,12,256]{3,2,1,0:T(8,128)(2,1)S(1)}, u32[]{:S(2)}, u32[]{:S(2)}) %all-to-all-start.2) | async-done | bytes 196640 | tf_op jit(solution)/shard_map/all_to_all | solution.py:26
  69.6 9.7 %collective-permute-done.2 = bf16[64,3,1,256]{0,3,2,1:T(8,128)(2,1)S(1)} collective-permute-done((bf16[64,3,1,256]{0,3,2,1:T(8,128)(2,1)S(1)}, bf16[64,3,1,256]{0,3,2,1:T(8,128)(2,1)S(1)}, u32[]{:S(2)}, u32[]{:S(2)}) %collective-permute-start.2) | collective-permute-done | bytes 98336 | tf_op jit(solution)/shard_map/ppermute | solution.py:18
  85.5 9.0 %all-to-all-done.3 = bf16[32,2,1536]{2,1,0:T(2,128)(2,1)S(1)} async-done(((bf16[32,2,1536]{2,1,0:T(2,128)(2,1)}), bf16[32,2,1536]{2,1,0:T(2,128)(2,1)S(1)}, u32[]{:S(2)}, u32[]{:S(2)}) %all-to-all-start.3) | async-done | bytes 196640 | tf_op jit(solution)/shard_map/all_to_all | solution.py:48
  95.1 8.6 %all_gather.16 = bf16[4,3,4,512]{3,2,1,0:T(4,128)(2,1)S(1)} all-gather(bf16[1,3,4,512]{3,2,1,0:T(4,128)(2,1)S(1)} %reshape.420), channel_id=1, replica_groups=mesh['face'=4,'tile'=32] {'face'}, dimensions={0}, use_global_device_ids=true | all-gather | bytes 61440 | tf_op jit(solution)/shard_map/all_gather | solution.py:57
  109.8 7.3 %collective-permute-start.3 = (bf16[64,3,1,256]{0,3,2,1:T(8,128)(2,1)}, bf16[64,3,1,256]{0,3,2,1:T(8,128)(2,1)}, u32[]{:S(2)}, u32[]{:S(2)}) collective-permute-start(bf16[64,3,1,256]{0,3,2,1:T(8,128)(2,1)} %get-tuple-element.108), channel_id=1, source_target_pairs={{1,0},{2,1},{3,2},{4,3},{5,4},{6,5},{7,6},{8,7},{9,8},{10,9},{11,1... | collective-permute-start | bytes 294920 | tf_op jit(solution)/shard_map/ppermute | solution.py:19
  178.2 8.4 %convert_reduce_fusion = f32[64,3,4,128]{0,3,2,1:T(8,128)S(1)} fusion(bf16[64,1,4,2,128,2]{0,5,4,3,2,1:T(2,128)(2,1)S(1)} %bitcast.592, bf16[64,1,4,2,128,2]{0,5,4,3,2,1:T(2,128)(2,1)S(1)} %bitcast.596, bf16[64,1,4,2,128,2]{0,5,4,3,2,1:T(2,128)(2,1)S(1)} %bitcast.600), kind=kLoop, calls=%fused_computation.27 | loop fusion | flops 1474560 | bytes 1179648 | tf_op jit(solution)/shard_map/reduce_sum | solution.py:151
  189.7 7.0 %collective-permute-start.5 = (bf16[64,3,1,256]{0,3,2,1:T(8,128)(2,1)}, bf16[64,3,1,256]{0,3,2,1:T(8,128)(2,1)}, u32[]{:S(2)}, u32[]{:S(2)}) collective-permute-start(bf16[64,3,1,256]{0,3,2,1:T(8,128)(2,1)} %get-tuple-element.104), channel_id=1, source_target_pairs={{1,0},{2,1},{3,2},{4,3},{5,4},{6,5},{7,6},{8,7},{9,8},{10,9},{11,1... | collective-permute-start | bytes 294920 | tf_op jit(solution)/shard_map/ppermute | solution.py:19
  204.7 6.7 %all-to-all-done.7 = bf16[32,2,768]{2,1,0:T(2,128)(2,1)S(1)} async-done(((bf16[32,2,768]{2,1,0:T(2,128)(2,1)}), bf16[32,2,768]{2,1,0:T(2,128)(2,1)S(1)}, u32[]{:S(2)}, u32[]{:S(2)}) %all-to-all-start.7) | async-done | bytes 98336 | tf_op jit(solution)/shard_map/all_to_all | solution.py:48
  216.0 9.8 %all_gather.18 = bf16[4,3,4,256]{3,2,1,0:T(4,128)(2,1)S(1)} all-gather(bf16[1,3,4,256]{3,2,1,0:T(4,128)(2,1)S(1)} %reshape.430), channel_id=1, replica_groups=mesh['face'=4,'tile'=32] {'face'}, dimensions={0}, use_global_device_ids=true | all-gather | bytes 30720 | tf_op jit(solution)/shard_map/all_gather | solution.py:57
  227.4 9.5 %all-to-all-start.8 = ((bf16[32,1,12,256]{3,2,1,0:T(8,128)(2,1)}), bf16[32,1,12,256]{3,2,1,0:T(8,128)(2,1)S(1)}, u32[]{:S(2)}, u32[]{:S(2)}) async-start(bf16[32,1,12,256]{3,2,1,0:T(8,128)(2,1)} %broadcast_in_dim.123), calls=%async_computation.8 | async-start | bytes 524288 | tf_op jit(solution)/shard_map/all_to_all | solution.py:26
  237.6 5.8 %all_gather.17 = bf16[4,3,4,512]{3,2,1,0:T(4,128)(2,1)S(1)} all-gather(bf16[1,3,4,512]{3,2,1,0:T(4,128)(2,1)S(1)} %reshape.425), channel_id=1, replica_groups=mesh['face'=4,'tile'=32] {'face'}, dimensions={0}, use_global_device_ids=true | all-gather | bytes 61440 | tf_op jit(solution)/shard_map/all_gather | solution.py:57
  285.3 6.7 %collective-permute-start.9 = (bf16[64,3,1,128]{0,3,2,1:T(8,128)(2,1)}, bf16[64,3,1,128]{0,3,2,1:T(8,128)(2,1)}, u32[]{:S(2)}, u32[]{:S(2)}) collective-permute-start(bf16[64,3,1,128]{0,3,2,1:T(8,128)(2,1)} %get-tuple-element.170), channel_id=1, source_target_pairs={{1,0},{2,1},{3,2},{4,3},{5,4},{6,5},{7,6},{8,7},{9,8},{10,9},{11,1... | collective-permute-start | bytes 147464 | tf_op jit(solution)/shard_map/ppermute | solution.py:19
  299.8 8.7 %all-to-all-done.9 = bf16[32,2,768]{2,1,0:T(2,128)(2,1)S(1)} async-done(((bf16[32,2,768]{2,1,0:T(2,128)(2,1)}), bf16[32,2,768]{2,1,0:T(2,128)(2,1)S(1)}, u32[]{:S(2)}, u32[]{:S(2)}) %all-to-all-start.9) | async-done | bytes 98336 | tf_op jit(solution)/shard_map/all_to_all | solution.py:48
  313.9 9.6 %all_gather.19 = bf16[4,3,4,256]{3,2,1,0:T(4,128)(2,1)S(1)} all-gather(bf16[1,3,4,256]{3,2,1,0:T(4,128)(2,1)S(1)} %reshape.435), channel_id=1, replica_groups=mesh['face'=4,'tile'=32] {'face'}, dimensions={0}, use_global_device_ids=true | all-gather | bytes 30720 | tf_op jit(solution)/shard_map/all_gather | solution.py:57
  325.0 10.7 %all-to-all-start.10 = ((bf16[32,1,12,256]{3,2,1,0:T(8,128)(2,1)}), bf16[32,1,12,256]{3,2,1,0:T(8,128)(2,1)}, u32[]{:S(2)}, u32[]{:S(2)}) async-start(bf16[32,1,12,256]{3,2,1,0:T(8,128)(2,1)} %broadcast_in_dim.124), calls=%async_computation.10 | async-start | bytes 524288 | tf_op jit(solution)/shard_map/all_to_all | solution.py:26
  345.6 7.6 %all-to-all-start = ((f32[32,2,2,256]{3,2,1,0:T(2,128)}), f32[32,2,2,256]{3,2,1,0:T(2,128)}, u32[]{:S(2)}, u32[]{:S(2)}) async-start(f32[32,2,2,256]{3,2,1,0:T(2,128)} %bitcast.9), calls=%async_computation | async-start | bytes 262144 | tf_op jit(solution)/shard_map/all_to_all | solution.py:183
  360.5 6.2 %reshape.440 = bf16[64,3,12,260]{0,3,2,1:T(8,128)(2,1)} reshape(bf16[64,3,12,130,2]{0,4,3,2,1:T(2,128)(2,1)} %broadcast_in_dim.126) | data formatting | bytes 2396160 | tf_op jit(solution)/shard_map/reshape | solution.py:106
  381.7 59.2 %while.10 = (s32[]{:T(128)}, f32[32,2,2,256]{3,2,1,0:T(2,128)}, f32[32,2,2,256]{3,2,1,0:T(2,128)}, bf16[32,2,4,256]{3,2,1,0:T(4,128)(2,1)S(1)}, f32[64,6]{0,1:T(8,128)S(1)}, /*index=5*/f32[64]{0:T(128)S(1)}, s32[]{:T(128)}) while((s32[]{:T(128)}, f32[32,2,2,256]{3,2,1,0:T(2,128)}, f32[32,2,2,256]{3,2,1,0:T(2,128)}, ...), condition=%wide.region_4.7_spmd, body=%wide.region_3.6_spmd.sunk | while | flops 3021314 | bytes 321377 | solution.py:125
  441.0 9.4 %all-to-all-start.11 = ((f32[32,2,2,256]{3,2,1,0:T(2,128)}), f32[32,2,2,256]{3,2,1,0:T(2,128)S(1)}, u32[]{:S(2)}, u32[]{:S(2)}) async-start(f32[32,2,2,256]{3,2,1,0:T(2,128)} %get-tuple-element.36), calls=%async_computation.11 | async-start | bytes 262144 | tf_op jit(solution)/shard_map/all_to_all | solution.py:198
  452.3 7.0 %all-to-all-done.11 = f32[32,2,2,256]{3,2,1,0:T(2,128)S(1)} async-done(((f32[32,2,2,256]{3,2,1,0:T(2,128)}), f32[32,2,2,256]{3,2,1,0:T(2,128)S(1)}, u32[]{:S(2)}, u32[]{:S(2)}) %all-to-all-start.11) | async-done | bytes 131104 | tf_op jit(solution)/shard_map/all_to_all | solution.py:198
  (752 shorter events, 270.8 us)
Async XLA Ops:
  0.6 380.4 %copy-start = (bf16[12,64]{1,0:T(8,128)(2,1)S(1)}, bf16[12,64]{1,0:T(8,128)(2,1)}, u32[]{:S(2)}) copy-start(bf16[12,64]{1,0:T(8,128)(2,1)} %param.27) | copy-start | bytes 4612
  2.0 12.2 %collective-permute-start = (bf16[32,3,1,256]{3,0,2,1:T(8,128)(2,1)S(1)}, bf16[32,3,1,256]{3,0,2,1:T(8,128)(2,1)S(1)}, u32[]{:S(2)}, u32[]{:S(2)}) collective-permute-start(bf16[32,3,1,256]{3,0,2,1:T(8,128)(2,1)S(1)} %copy.592), channel_id=1, source_target_pairs={{0,1},{1,2},{2,3},{3,4},{4,5},{5,6},{6,7},{7,8},{8,9},{9,10},{10,1... | collective-permute-start | bytes 147464 | tf_op jit(solution)/shard_map/ppermute | solution.py:18
  4.8 50.6 %collective-permute-start.1 = (bf16[32,3,1,256]{3,0,2,1:T(8,128)(2,1)}, bf16[32,3,1,256]{3,0,2,1:T(8,128)(2,1)}, u32[]{:S(2)}, u32[]{:S(2)}) collective-permute-start(bf16[32,3,1,256]{3,0,2,1:T(8,128)(2,1)} %copy.591), channel_id=1, source_target_pairs={{1,0},{2,1},{3,2},{4,3},{5,4},{6,5},{7,6},{8,7},{9,8},{10,9},{11,1... | collective-permute-start | bytes 147464 | tf_op jit(solution)/shard_map/ppermute | solution.py:19
  13.7 90.7 %copy-start.69 = (pred[12]{0:T(512)(128)(4,1)}, pred[12]{0:T(512)(128)(4,1)S(1)}, u32[]{:S(2)}) copy-start(pred[12]{0:T(512)(128)(4,1)S(1)} %get-tuple-element.49) | copy-start | bytes 40
  16.3 13.0 %all-to-all-start.1 = ((bf16[32,2,768]{2,1,0:T(2,128)(2,1)}), bf16[32,2,768]{2,1,0:T(2,128)(2,1)S(1)}, u32[]{:S(2)}, u32[]{:S(2)}) async-start(bf16[32,2,768]{2,1,0:T(2,128)(2,1)} %reshape.504), calls=%async_computation.1 | async-start | bytes 196608 | tf_op jit(solution)/shard_map/all_to_all | solution.py:48
  38.9 14.0 %all-to-all-start.2 = ((bf16[32,1,12,256]{3,2,1,0:T(8,128)(2,1)}), bf16[32,1,12,256]{3,2,1,0:T(8,128)(2,1)S(1)}, u32[]{:S(2)}, u32[]{:S(2)}) async-start(bf16[32,1,12,256]{3,2,1,0:T(8,128)(2,1)} %broadcast_in_dim.119), calls=%async_computation.2 | async-start | bytes 524288 | tf_op jit(solution)/shard_map/all_to_all | solution.py:26
  68.8 10.5 %collective-permute-start.2 = (bf16[64,3,1,256]{0,3,2,1:T(8,128)(2,1)S(1)}, bf16[64,3,1,256]{0,3,2,1:T(8,128)(2,1)S(1)}, u32[]{:S(2)}, u32[]{:S(2)}) collective-permute-start(bf16[64,3,1,256]{0,3,2,1:T(8,128)(2,1)S(1)} %get-tuple-element.109), channel_id=1, source_target_pairs={{0,1},{1,2},{2,3},{3,4},{4,5},{5,6},{6,7},{7,8},{8,9},{9,10},{10,1... | collective-permute-start | bytes 294920 | tf_op jit(solution)/shard_map/ppermute | solution.py:18
  81.4 13.1 %all-to-all-start.3 = ((bf16[32,2,1536]{2,1,0:T(2,128)(2,1)}), bf16[32,2,1536]{2,1,0:T(2,128)(2,1)S(1)}, u32[]{:S(2)}, u32[]{:S(2)}) async-start(bf16[32,2,1536]{2,1,0:T(2,128)(2,1)} %reshape.506), calls=%async_computation.3 | async-start | bytes 393216 | tf_op jit(solution)/shard_map/all_to_all | solution.py:48
  105.3 16.0 %all-to-all-start.4 = ((bf16[32,1,12,512]{3,2,1,0:T(8,128)(2,1)}), bf16[32,1,12,512]{3,2,1,0:T(8,128)(2,1)S(1)}, u32[]{:S(2)}, u32[]{:S(2)}) async-start(bf16[32,1,12,512]{3,2,1,0:T(8,128)(2,1)} %broadcast_in_dim.120), calls=%async_computation.4 | async-start | bytes 1048576 | tf_op jit(solution)/shard_map/all_to_all | solution.py:26
  109.8 17.7 %collective-permute-start.3 = (bf16[64,3,1,256]{0,3,2,1:T(8,128)(2,1)}, bf16[64,3,1,256]{0,3,2,1:T(8,128)(2,1)}, u32[]{:S(2)}, u32[]{:S(2)}) collective-permute-start(bf16[64,3,1,256]{0,3,2,1:T(8,128)(2,1)} %get-tuple-element.108), channel_id=1, source_target_pairs={{1,0},{2,1},{3,2},{4,3},{5,4},{6,5},{7,6},{8,7},{9,8},{10,9},{11,1... | collective-permute-start | bytes 294920 | tf_op jit(solution)/shard_map/ppermute | solution.py:19
  187.4 9.6 %collective-permute-start.6 = (bf16[64,3,1,128]{0,3,2,1:T(8,128)(2,1)S(1)}, bf16[64,3,1,128]{0,3,2,1:T(8,128)(2,1)S(1)}, u32[]{:S(2)}, u32[]{:S(2)}) collective-permute-start(bf16[64,3,1,128]{0,3,2,1:T(8,128)(2,1)S(1)} %get-tuple-element.183), channel_id=1, source_target_pairs={{0,1},{1,2},{2,3},{3,4},{4,5},{5,6},{6,7},{7,8},{8,9},{9,10},{10,1... | collective-permute-start | bytes 147464 | tf_op jit(solution)/shard_map/ppermute | solution.py:18
  189.4 13.3 %collective-permute-start.4 = (bf16[64,3,1,256]{0,3,2,1:T(8,128)(2,1)S(1)}, bf16[64,3,1,256]{0,3,2,1:T(8,128)(2,1)S(1)}, u32[]{:S(2)}, u32[]{:S(2)}) collective-permute-start(bf16[64,3,1,256]{0,3,2,1:T(8,128)(2,1)S(1)} %get-tuple-element.105), channel_id=1, source_target_pairs={{0,1},{1,2},{2,3},{3,4},{4,5},{5,6},{6,7},{7,8},{8,9},{9,10},{10,1... | collective-permute-start | bytes 294920 | tf_op jit(solution)/shard_map/ppermute | solution.py:18
  189.7 153.0 %collective-permute-start.5 = (bf16[64,3,1,256]{0,3,2,1:T(8,128)(2,1)}, bf16[64,3,1,256]{0,3,2,1:T(8,128)(2,1)}, u32[]{:S(2)}, u32[]{:S(2)}) collective-permute-start(bf16[64,3,1,256]{0,3,2,1:T(8,128)(2,1)} %get-tuple-element.104), channel_id=1, source_target_pairs={{1,0},{2,1},{3,2},{4,3},{5,4},{6,5},{7,6},{8,7},{9,8},{10,9},{11,1... | collective-permute-start | bytes 294920 | tf_op jit(solution)/shard_map/ppermute | solution.py:19
  196.7 52.4 %collective-permute-start.7 = (bf16[64,3,1,128]{0,3,2,1:T(8,128)(2,1)}, bf16[64,3,1,128]{0,3,2,1:T(8,128)(2,1)}, u32[]{:S(2)}, u32[]{:S(2)}) collective-permute-start(bf16[64,3,1,128]{0,3,2,1:T(8,128)(2,1)} %get-tuple-element.182), channel_id=1, source_target_pairs={{1,0},{2,1},{3,2},{4,3},{5,4},{6,5},{7,6},{8,7},{9,8},{10,9},{11,1... | collective-permute-start | bytes 147464 | tf_op jit(solution)/shard_map/ppermute | solution.py:19
  198.8 12.6 %all-to-all-start.7 = ((bf16[32,2,768]{2,1,0:T(2,128)(2,1)}), bf16[32,2,768]{2,1,0:T(2,128)(2,1)S(1)}, u32[]{:S(2)}, u32[]{:S(2)}) async-start(bf16[32,2,768]{2,1,0:T(2,128)(2,1)} %reshape.508), calls=%async_computation.7 | async-start | bytes 196608 | tf_op jit(solution)/shard_map/all_to_all | solution.py:48
  211.5 15.2 %all-to-all-start.5 = ((bf16[32,2,1536]{2,1,0:T(2,128)(2,1)}), bf16[32,2,1536]{2,1,0:T(2,128)(2,1)S(1)}, u32[]{:S(2)}, u32[]{:S(2)}) async-start(bf16[32,2,1536]{2,1,0:T(2,128)(2,1)} %reshape.512), calls=%async_computation.5 | async-start | bytes 393216 | tf_op jit(solution)/shard_map/all_to_all | solution.py:48
  227.4 19.4 %all-to-all-start.8 = ((bf16[32,1,12,256]{3,2,1,0:T(8,128)(2,1)}), bf16[32,1,12,256]{3,2,1,0:T(8,128)(2,1)S(1)}, u32[]{:S(2)}, u32[]{:S(2)}) async-start(bf16[32,1,12,256]{3,2,1,0:T(8,128)(2,1)} %broadcast_in_dim.123), calls=%async_computation.8 | async-start | bytes 524288 | tf_op jit(solution)/shard_map/all_to_all | solution.py:26
  284.8 9.2 %collective-permute-start.8 = (bf16[64,3,1,128]{0,3,2,1:T(8,128)(2,1)S(1)}, bf16[64,3,1,128]{0,3,2,1:T(8,128)(2,1)S(1)}, u32[]{:S(2)}, u32[]{:S(2)}) collective-permute-start(bf16[64,3,1,128]{0,3,2,1:T(8,128)(2,1)S(1)} %get-tuple-element.171), channel_id=1, source_target_pairs={{0,1},{1,2},{2,3},{3,4},{4,5},{5,6},{6,7},{7,8},{8,9},{9,10},{10,1... | collective-permute-start | bytes 147464 | tf_op jit(solution)/shard_map/ppermute | solution.py:18
  285.3 71.1 %collective-permute-start.9 = (bf16[64,3,1,128]{0,3,2,1:T(8,128)(2,1)}, bf16[64,3,1,128]{0,3,2,1:T(8,128)(2,1)}, u32[]{:S(2)}, u32[]{:S(2)}) collective-permute-start(bf16[64,3,1,128]{0,3,2,1:T(8,128)(2,1)} %get-tuple-element.170), channel_id=1, source_target_pairs={{1,0},{2,1},{3,2},{4,3},{5,4},{6,5},{7,6},{8,7},{9,8},{10,9},{11,1... | collective-permute-start | bytes 147464 | tf_op jit(solution)/shard_map/ppermute | solution.py:19
  295.8 12.6 %all-to-all-start.9 = ((bf16[32,2,768]{2,1,0:T(2,128)(2,1)}), bf16[32,2,768]{2,1,0:T(2,128)(2,1)S(1)}, u32[]{:S(2)}, u32[]{:S(2)}) async-start(bf16[32,2,768]{2,1,0:T(2,128)(2,1)} %reshape.510), calls=%async_computation.9 | async-start | bytes 196608 | tf_op jit(solution)/shard_map/all_to_all | solution.py:48
  309.3 15.0 %all-to-all-start.6 = ((bf16[32,1,12,512]{3,2,1,0:T(8,128)(2,1)}), bf16[32,1,12,512]{3,2,1,0:T(8,128)(2,1)S(1)}, u32[]{:S(2)}, u32[]{:S(2)}) async-start(bf16[32,1,12,512]{3,2,1,0:T(8,128)(2,1)} %broadcast_in_dim.121), calls=%async_computation.6 | async-start | bytes 1048576 | tf_op jit(solution)/shard_map/all_to_all | solution.py:26
  325.0 20.6 %all-to-all-start.10 = ((bf16[32,1,12,256]{3,2,1,0:T(8,128)(2,1)}), bf16[32,1,12,256]{3,2,1,0:T(8,128)(2,1)}, u32[]{:S(2)}, u32[]{:S(2)}) async-start(bf16[32,1,12,256]{3,2,1,0:T(8,128)(2,1)} %broadcast_in_dim.124), calls=%async_computation.10 | async-start | bytes 524288 | tf_op jit(solution)/shard_map/all_to_all | solution.py:26
  345.6 36.1 %all-to-all-start = ((f32[32,2,2,256]{3,2,1,0:T(2,128)}), f32[32,2,2,256]{3,2,1,0:T(2,128)}, u32[]{:S(2)}, u32[]{:S(2)}) async-start(f32[32,2,2,256]{3,2,1,0:T(2,128)} %bitcast.9), calls=%async_computation | async-start | bytes 262144 | tf_op jit(solution)/shard_map/all_to_all | solution.py:183
  441.0 18.3 %all-to-all-start.11 = ((f32[32,2,2,256]{3,2,1,0:T(2,128)}), f32[32,2,2,256]{3,2,1,0:T(2,128)S(1)}, u32[]{:S(2)}, u32[]{:S(2)}) async-start(f32[32,2,2,256]{3,2,1,0:T(2,128)} %get-tuple-element.36), calls=%async_computation.11 | async-start | bytes 262144 | tf_op jit(solution)/shard_map/all_to_all | solution.py:198
  (77 other events, 542.0 us)
where the time goes:
time: 469 us; the launch traced here: 460 us
  local copies, waits for them, and re-layouts  142 us (30%)
  starting transfers between devices  102 us (22%)
  waiting for transfers between devices  69.8 us (15%)
  other arithmetic  58.2 us (12%)
  matrix products  42.8 us (9%)
  blocking collectives  41.5 us (9%)
    concatenate x51, local copies, waits for them, and re-layouts, convolve(): jnp.concatenate([padded[:, face_index, row_shift:row_shift + stripe_rows,...  47.9 us
    all_gather x5, blocking collectives, pad_field(): grouped = lax.all_gather(seam_piece, 'face', axis=0, tiled=True)  41.5 us
    all_to_all x5, waiting for transfers between devices, pad_field(): lax.all_to_all(edge_pieces, 'tile', split_axis=3, concat_axis=3, tiled=True)  33.1 us
    all_to_all x5, starting transfers between devices, sent_to_all(): return lax.all_to_all(copies, axis, split_axis=0, concat_axis=0, tiled=True)  32.1 us
    ppermute x5, starting transfers between devices, extended(): after = lax.ppermute(initial, axis, down)  28.3 us
    dot_general x36, matrix products, convolve(): jnp.dot(weight[row_shift], tap_rows.reshape(3 * channels, stripe_rows * f...  25.2 us
    squeeze x32, local copies, waits for them, and re-layouts, ocean_blocks(): lax.map(lambda pair: ocean_update(pair[0], pair[1], ocean_in, ocean_out),...  21.7 us
    all_to_all x5, starting transfers between devices, pad_field(): lax.all_to_all(edge_pieces, 'tile', split_axis=3, concat_axis=3, tiled=True)  19.6 us
  transfers between devices with their start and end apart: 22, of which 11 were waited for; matrix products, arithmetic and copies ran while one was open for 23% of the time, Pallas kernels for 0%

commit v1 on v0

v1 whole, which is shorter than its diff:
```python
import functools

import jax
import jax.numpy as jnp
from jax import lax
from jax.experimental import pallas as pl
from jax.experimental.pallas import tpu as pltpu
from jax.sharding import PartitionSpec as P

MESH = pl.DeviceIdType.MESH
BF = jnp.bfloat16
F32 = jnp.float32
C = 64
OUT_VARS = 8
FLUX_CH = 4
OCEAN_CH = 2
NT = (((1,), (1,)), ((), ()))
TN = (((0,), (0,)), ((), ()))

HALO_SEND, HALO_UP, HALO_DOWN, SCAT_SEND, SCAT_TOP, SCAT_BOT = range(6)
TAB_SEND, TAB_RECV, PICK_SEND, PICK_RECV, SEM_COLS = 6, 7, 8, 10, 12
HALO_DOWN_SEND = 11


def iota(shape, dim):
    return lax.broadcasted_iota(jnp.int32, shape, dim)


def drain(ref, sem):
    pltpu.make_async_copy(ref, ref, sem).wait()


class Level:
    def __init__(self, rows, side, body, sems, bufs, sel):
        self.rows, self.side, self.body, self.sems = rows, side, body, sems
        self.scat, self.scat_in, self.tab, self.tabs, self.pick, self.gath = bufs
        self.sel = sel


def kernel(
    groups,
    tiles,
    rows,
    faces,
    seam_ref,
    inv_ref,
    slot_ref,
    atmos_ref,
    land_ref,
    held_ref,
    w1_ref,
    w2_ref,
    w3_ref,
    w4_ref,
    w5_ref,
    head_ref,
    oin_ref,
    oout_ref,
    out_ref,
    sea_ref,
    body1,
    body2,
    body3,
    bodys,
    body4,
    bodyc,
    sel_f,
    sel_c,
    up_mat,
    down_mat,
    pred,
    flux,
    visit,
    sea_out,
    sea_in,
    *rest,
):
    bufs, (sems, misc) = rest[:-2], rest[-2:]
    f = lax.axis_index("face")
    t = lax.axis_index("tile")
    side = rows * tiles
    half_rows, half_side = rows // 2, side // 2
    is_top, is_bot = t == 0, t == tiles - 1
    last = tiles - 1

    load = pltpu.make_async_copy(
        atmos_ref, body1.at[:, pl.ds(C, rows * C), pl.ds(0, side)], misc.at[0]
    )
    load.start()

    levels = []
    for number, (n, s, body, sel) in enumerate(
        (
            (rows, side, body1, sel_f),
            (rows, side, body2, sel_f),
            (half_rows, half_side, body3, sel_c),
            (rows, side, bodys, sel_f),
            (half_rows, half_side, body4, sel_c),
        )
    ):
        levels.append(Level(n, s, body, sems.at[number], bufs[6 * number : 6 * number + 6], sel))

    for n, s, sel in ((rows, side, sel_f), (half_rows, half_side, sel_c)):
        shape = (tiles * 16, s)
        q, x = iota(shape, 0), iota(shape, 1)
        k = q % 16
        cell = (q // 16) * n + k - 1
        inner = (k >= 1) & (k <= n)
        sel[0] = jnp.where((x == cell) & (k <= n + 1), 1.0, 0.0).astype(BF)
        sel[1] = jnp.where((x == cell) & inner, 1.0, 0.0).astype(BF)
        sel[2] = jnp.where((x == s - 1 - cell) & inner, 1.0, 0.0).astype(BF)
    shape = (half_side, side)
    up_mat[...] = jnp.where(iota(shape, 1) // 2 == iota(shape, 0), 1.0, 0.0).astype(BF)
    shape = (side, half_side)
    down_mat[...] = jnp.where(iota(shape, 0) // 2 == iota(shape, 1), 0.25, 0.0).astype(BF)

    barrier = pltpu.get_barrier_semaphore()

    def greet(d, carry):
        peer = lax.rem(t + d, tiles)
        pl.semaphore_signal(barrier, inc=1, device_id=(f, peer), device_id_type=MESH)
        return carry

    lax.fori_loop(1, tiles, greet, 0)
    for d in range(1, groups):
        g = lax.rem(f + d, groups)
        pl.semaphore_signal(barrier, inc=1, device_id=(g, t), device_id_type=MESH)
        pl.semaphore_signal(barrier, inc=1, device_id=(g, last - t), device_id_type=MESH)
    pl.semaphore_wait(barrier, tiles - 1 + 2 * (groups - 1))

    def remote(src, dst, send, recv, device):
        return pltpu.make_async_remote_copy(
            src_ref=src,
            dst_ref=dst,
            send_sem=send,
            recv_sem=recv,
            device_id=device,
            device_id_type=MESH,
        )

    def halo_up(lv):
        n, s = lv.rows, lv.side
        return remote(
            lv.body.at[:, pl.ds(C, C), pl.ds(0, s)],
            lv.body.at[:, pl.ds((n + 1) * C, C), pl.ds(0, s)],
            lv.sems.at[HALO_SEND],
            lv.sems.at[HALO_DOWN],
            (f, jnp.maximum(t - 1, 0)),
        )

    def halo_down(lv):
        n, s = lv.rows, lv.side
        return remote(
            lv.body.at[:, pl.ds(n * C, C), pl.ds(0, s)],
            lv.body.at[:, pl.ds(0, C), pl.ds(0, s)],
            lv.sems.at[HALO_DOWN_SEND],
            lv.sems.at[HALO_UP],
            (f, jnp.minimum(t + 1, last)),
        )

    def scatter_piece(lv, which, dst):
        return remote(
            lv.scat.at[dst],
            lv.scat_in.at[which],
            lv.sems.at[SCAT_SEND],
            lv.sems.at[SCAT_TOP + which],
            (f, dst),
        )

    def begin_rows(lv):
        n, s = lv.rows, lv.side

        @pl.when(jnp.logical_not(is_top))
        def _():
            halo_up(lv).start()

        @pl.when(jnp.logical_not(is_bot))
        def _():
            halo_down(lv).start()

        for which, cond in ((0, is_top), (1, is_bot)):

            @pl.when(cond)
            def _(which=which):
                for j in range(faces):
                    start = C if which == 0 else n * C
                    edge = lv.body[j, pl.ds(start, C), pl.ds(0, s)]
                    zero = jnp.zeros_like(edge)
                    both = jnp.concatenate([edge, zero] if which == 0 else [zero, edge], axis=0)
                    piece = lax.dot_general(
                        lv.sel[0], both, NT, preferred_element_type=F32
                    ).astype(BF)
                    lv.scat[:, j] = piece.reshape(tiles, 16, 2 * C)
                own = 0 if which == 0 else last
                lv.scat_in[which] = lv.scat[own]

                def send(d, carry):
                    scatter_piece(lv, which, lax.rem(own + d, tiles)).start()
                    return carry

                lax.fori_loop(1, tiles, send, 0)

    def end_rows(lv):
        @pl.when(jnp.logical_not(is_top))
        def _():
            drain(lv.body.at[:, pl.ds(0, C), pl.ds(0, lv.side)], lv.sems.at[HALO_UP])
            drain(lv.scat_in.at[0], lv.sems.at[SCAT_TOP])

        @pl.when(jnp.logical_not(is_bot))
        def _():
            n = lv.rows
            drain(lv.body.at[:, pl.ds((n + 1) * C, C), pl.ds(0, lv.side)], lv.sems.at[HALO_DOWN])
            drain(lv.scat_in.at[1], lv.sems.at[SCAT_BOT])

    def table_copy(lv, d):
        mirrored = d // groups
        g = lax.rem(f + d % groups, groups)
        peer = last - t if mirrored else t
        width = 2 * faces
        return remote(
            lv.tab,
            lv.tabs.at[pl.ds((mirrored * groups + f) * width, width)],
            lv.sems.at[TAB_SEND],
            lv.sems.at[TAB_RECV],
            (g, peer),
        )

    def begin_tables(lv):
        n, s = lv.rows, lv.side
        shape = (32, s)
        row, lane = iota(shape, 0), iota(shape, 1)

        def one_face(j, carry):
            total = jnp.zeros((32, C), F32)
            for k in range(n + 2):
                pick = ((row == k) & (lane == 0)) | ((row == 16 + k) & (lane == s - 1))
                data = lv.body[j, pl.ds(k * C, C), pl.ds(0, s)]
                if k == 0:
                    data = jnp.where(is_top, jnp.zeros_like(data), data)
                if k == n + 1:
                    data = jnp.where(is_bot, jnp.zeros_like(data), data)
                total += lax.dot_general(
                    jnp.where(pick, 1.0, 0.0).astype(BF), data, NT, preferred_element_type=F32
                )
            lv.tab[2 * j + 1] = jnp.concatenate([total[:16], total[16:]], axis=1).astype(BF)
            lv.tab[2 * j] = lv.scat_in[0, j] + lv.scat_in[1, j]
            return carry

        lax.fori_loop(0, faces, one_face, 0)
        for d in range(1, 2 * groups):
            table_copy(lv, d).start()
        lv.tabs[pl.ds(f * 2 * faces, 2 * faces)] = lv.tab[...]

    def end_tables(lv):
        drain(lv.tabs.at[pl.ds(0, (2 * groups - 1) * 2 * faces)], lv.sems.at[TAB_RECV])

    def row_copy(lv, which):
        return remote(
            lv.pick.at[which],
            lv.gath.at[t],
            lv.sems.at[PICK_SEND + which],
            lv.sems.at[PICK_RECV],
            (f, 0 if which == 0 else last),
        )

    def seam(j, s):
        at = (f * faces + j) * 4 + s
        return seam_ref[at, 0], seam_ref[at, 1]

    def begin_strips(lv):
        for which, cond in ((0, is_top), (1, is_bot)):
            for j in range(faces):
                p, _ = seam(j, which)
                lv.pick[which, j] = lv.tabs[p // 2]

            @pl.when(jnp.logical_not(cond))
            def _(which=which):
                row_copy(lv, which).start()

            @pl.when(cond)
            def _(which=which):
                lv.gath[0 if which == 0 else last] = lv.pick[which]

    def column_strips(lv, j, store):
        n = lv.rows
        shape = (16, 128)
        k, lane = iota(shape, 0), iota(shape, 1)
        total = jnp.zeros((C, 128), F32)
        for s in (2, 3):
            p, rev = seam(j, s)
            piece = lv.tabs[rev * (groups * 2 * faces) + p // 2]
            kk = jnp.where(rev == 1, n + 1 - k, k)
            good = (kk >= jnp.where(is_top, 1, 0)) & (kk <= jnp.where(is_bot, n, n + 1))
            want = (2 * kk + 127) % 128 if s == 2 else 2 * kk
            chosen = jnp.where(good & (lane == want), 1.0, 0.0).astype(BF)
            both = lax.dot_general(piece, chosen, TN, preferred_element_type=F32)
            total += jnp.where(p % 2 == 1, both[C:], both[:C])
        store(j, total)

    def store_columns(lv):
        def store(j, total):
            for k in range(lv.rows + 2):
                lv.body[j, pl.ds(k * C, C), pl.ds(lv.side, 128)] = pltpu.roll(
                    total, (128 - 2 * k) % 128, 1
                ).astype(BF)

        def one_face(j, carry):
            column_strips(lv, j, store)
            return carry

        lax.fori_loop(0, faces, one_face, 0)

    def end_strips(lv):
        n, s = lv.rows, lv.side
        for which, cond in ((0, is_top), (1, is_bot)):

            @pl.when(cond)
            def _(which=which):
                drain(lv.gath.at[pl.ds(0, tiles - 1)], lv.sems.at[PICK_RECV])
                for j in range(faces):
                    p, rev = seam(j, which)
                    pieces = lv.gath[:, j].reshape(tiles * 16, 2 * C)
                    both = lax.dot_general(
                        pieces, lv.sel[1 + rev], TN, preferred_element_type=F32
                    )
                    strip = jnp.where(p % 2 == 1, both[C:], both[:C])
                    at = 0 if which == 0 else (n + 1) * C
                    lv.body[j, pl.ds(at, C), pl.ds(0, s)] = strip.astype(BF)

    def finish_sends(lv):
        n, s = lv.rows, lv.side

        @pl.when(jnp.logical_not(is_top))
        def _():
            halo_up(lv).wait_send()
            row_copy(lv, 0).wait_send()

        @pl.when(jnp.logical_not(is_bot))
        def _():
            halo_down(lv).wait_send()
            row_copy(lv, 1).wait_send()

        @pl.when(is_top | is_bot)
        def _():
            drain(lv.scat.at[pl.ds(0, tiles - 1)], lv.sems.at[SCAT_SEND])

        drain(lv.tabs.at[pl.ds(0, (2 * groups - 1) * 2 * faces)], lv.sems.at[TAB_SEND])

    def taps(product, s):
        wide = s + 128
        mid = product[C : 2 * C, :s]
        left = pltpu.roll(product[:C], 1, 1)[:, :s]
        right = pltpu.roll(product[2 * C :], wide - 1, 1)[:, :s]
        return mid + left + right

    def conv(lv, w_ref, target):
        n, s = lv.rows, lv.side

        def one_row(i, carry):
            j, r = i // n, i % n
            window = lv.body[j, pl.ds(pl.multiple_of(r * C, C), 3 * C), :]
            product = jnp.dot(w_ref[...], window, preferred_element_type=F32)
            made = jax.nn.gelu(taps(product, s)).astype(BF)
            target[j, pl.ds(pl.multiple_of(r * C + C, C), C), pl.ds(0, s)] = made
            return carry

        lax.fori_loop(0, faces * n, one_row, 0)

    def state_copy(d):
        dst = lax.rem(t + d, tiles)
        return remote(
            held_ref.at[pl.ds(2 * dst, 2)],
            visit.at[pl.ds(2 * t, 2)],
            misc.at[1],
            misc.at[2],
            (f, dst),
        )

    def sea_copy(d):
        dst = lax.rem(t + d, tiles)
        return remote(
            sea_out.at[pl.ds(2 * dst, 2)],
            sea_in.at[pl.ds(2 * t, 2)],
            misc.at[3],
            misc.at[4],
            (f, dst),
        )

    def start_all(copy):
        def body(d, carry):
            copy(d).start()
            return carry

        lax.fori_loop(1, tiles, body, 0)

    lv1, lv2, lv3, lvs, lv4 = levels
    load.wait()
    begin_rows(lv1)
    start_all(state_copy)
    visit[pl.ds(2 * t, 2)] = held_ref[pl.ds(2 * t, 2)]

    def exchange(lv):
        end_rows(lv)
        begin_tables(lv)
        end_tables(lv)
        begin_strips(lv)

    exchange(lv1)
    store_columns(lv1)
    end_strips(lv1)
    conv(lv1, w1_ref, body2)

    begin_rows(lv2)
    exchange(lv2)
    store_columns(lv2)
    end_strips(lv2)
    conv(lv2, w2_ref, bodys)

    def pool(i, carry):
        j, q = i // half_rows, i % half_rows
        pair = bodys[j, pl.ds(pl.multiple_of((2 * q + 1) * C, C), 2 * C), pl.ds(0, side)]
        summed = jnp.dot(pair, down_mat[...], preferred_element_type=F32)
        at = pl.ds(pl.multiple_of((q + 1) * C, C), C)
        body3[j, at, pl.ds(0, half_side)] = (summed[:C] + summed[C:]).astype(BF)
        return carry

    lax.fori_loop(0, faces * half_rows, pool, 0)

    begin_rows(lv3)
    begin_rows(lvs)
    exchange(lv3)
    store_columns(lv3)
    end_strips(lv3)
    conv(lv3, w3_ref, body4)

    begin_rows(lv4)
    exchange(lvs)
    store_columns(lvs)
    exchange(lv4)
    end_strips(lvs)

    def store_coarse(j, total):
        for k in range(rows + 2):
            bodyc[j, pl.ds(k * C, C), pl.ds(side, 128)] = pltpu.roll(
                total, (128 - 2 * ((k + 1) // 2)) % 128, 1
            ).astype(BF)

    def coarse_columns(j, carry):
        column_strips(lv4, j, store_coarse)
        return carry

    lax.fori_loop(0, faces, coarse_columns, 0)
    end_strips(lv4)

    def widen(j, carry):
        for q in range(half_rows + 2):
            made = jnp.dot(
                body4[j, pl.ds(q * C, C), :], up_mat[...], preferred_element_type=F32
            ).astype(BF)
            for k in (2 * q - 1, 2 * q):
                if 0 <= k <= rows + 1:
                    bodyc[j, pl.ds(k * C, C), pl.ds(0, side)] = made
        return carry

    lax.fori_loop(0, faces, widen, 0)

    def decode(i, carry):
        j, r = i // rows, i % rows
        window = pl.ds(pl.multiple_of(r * C, C), 3 * C)
        product = jnp.dot(w4_ref[...], bodys[j, window, :], preferred_element_type=F32)
        product += jnp.dot(w5_ref[...], bodyc[j, window, :], preferred_element_type=F32)
        decoded = jax.nn.gelu(taps(product, side)).astype(BF)
        head = jnp.dot(head_ref[...], decoded, preferred_element_type=F32)
        state = body1[j, pl.ds(pl.multiple_of(r * C + C, C), 16), pl.ds(0, side)]
        pred[i] = state[:OUT_VARS].astype(F32) + head[:OUT_VARS]
        ocean = jnp.broadcast_to(land_ref[i] == 1, (8, side))
        flux[i] = jnp.where(ocean, head[OUT_VARS:], 0.0).astype(BF).astype(F32)
        return carry

    lax.fori_loop(0, faces * rows, decode, 0)
    flux[faces * rows] = jnp.zeros((8, side), F32)

    drain(visit.at[pl.ds(0, 2 * (tiles - 1))], misc.at[2])

    def ocean(n, carry):
        old = visit[n]
        stacked = jnp.concatenate([old, jnp.zeros((6, side), F32)], axis=0) + flux[inv_ref[n]]
        hidden = jax.nn.gelu(
            jnp.dot(
                oin_ref[...],
                stacked,
                preferred_element_type=F32,
                precision=lax.Precision.HIGHEST,
            )
        )
        moved = jnp.sum(oout_ref[...] * hidden, axis=0, keepdims=True)
        sea_out[n] = old[:1] + moved
        return carry

    lax.fori_loop(0, 2 * tiles, ocean, 0)
    start_all(sea_copy)
    sea_in[pl.ds(2 * t, 2)] = sea_out[pl.ds(2 * t, 2)]

    def surface(i, carry):
        sea = jnp.broadcast_to(sea_out[slot_ref[i]], (8, side))
        wet = jnp.broadcast_to(land_ref[i] == 1, (8, side)) & (iota((8, side), 0) == 0)
        out_ref[i] = jnp.where(wet, sea, pred[i])
        return carry

    lax.fori_loop(0, faces * rows, surface, 0)
    drain(sea_in.at[pl.ds(0, 2 * (tiles - 1))], misc.at[4])
    sea_ref[...] = sea_in[...]

    for lv in levels:
        finish_sends(lv)
    drain(held_ref.at[pl.ds(0, 2 * (tiles - 1))], misc.at[1])
    drain(sea_out.at[pl.ds(0, 2 * (tiles - 1))], misc.at[3])


def stacked_weight(weight):
    taps, made, wide = weight.shape
    channels = wide // 3
    folded = jnp.transpose(weight.reshape(taps, made, 3, channels), (2, 1, 0, 3))
    if channels < C:
        folded = jnp.pad(folded, ((0, 0), (0, 0), (0, 0), (0, C - channels)))
    pieces = []
    for at in range(0, folded.shape[3], C):
        pieces.append(folded[..., at : at + C].reshape(3 * made, taps * C))
    return pieces


def on_device(
    atmos_state,
    land_sea,
    owners,
    seam_table,
    ocean_state,
    conv_input,
    conv_encode,
    conv_coarse,
    conv_decode,
    output_head,
    ocean_in,
    ocean_out,
):
    channels, faces, rows, side = atmos_state.shape
    groups, tiles = lax.axis_size("face"), lax.axis_size("tile")
    count = faces * rows
    slots = ocean_state.shape[2]
    atmos = jnp.pad(jnp.transpose(atmos_state, (1, 2, 0, 3)), ((0, 0), (0, 0), (0, C - channels), (0, 0)))
    atmos = atmos.reshape(faces, rows * C, side)
    land = land_sea.reshape(count, 1, side)
    owner_ids = owners[:, 0]
    same = owner_ids[:, None] == owner_ids[None, :]
    earlier = jnp.arange(count)[None, :] < jnp.arange(count)[:, None]
    rank = jnp.sum((same & earlier).astype(jnp.int32), axis=1)
    slot = owner_ids * (slots // tiles) + rank
    hits = jnp.arange(slots)[:, None] == slot[None, :]
    inverse = count + jnp.sum(
        jnp.where(hits, jnp.arange(count)[None, :] - count, 0), axis=1
    )
    held = ocean_state[0, 0]
    (w1,) = stacked_weight(conv_input)
    (w2,) = stacked_weight(conv_encode)
    (w3,) = stacked_weight(conv_coarse)
    w4, w5 = stacked_weight(conv_decode)
    gap = jnp.zeros((OCEAN_CH, output_head.shape[1]), output_head.dtype)
    head = jnp.concatenate([output_head[:OUT_VARS], gap, output_head[OUT_VARS:], gap], axis=0)
    oin = jnp.pad(ocean_in, ((0, 0), (0, 8 - ocean_in.shape[1])))
    oout = ocean_out[:, None]

    half_rows, half_side = rows // 2, side // 2
    vmem = pltpu.VMEM
    scratch = [
        vmem((faces, (rows + 2) * C, side + 128), BF),
        vmem((faces, (rows + 2) * C, side + 128), BF),
        vmem((faces, (half_rows + 2) * C, half_side + 128), BF),
        vmem((faces, (rows + 2) * C, side + 128), BF),
        vmem((faces, (half_rows + 2) * C, half_side), BF),
        vmem((faces, (rows + 2) * C, side + 128), BF),
        vmem((3, tiles * 16, side), BF),
        vmem((3, tiles * 16, half_side), BF),
        vmem((half_side, side), BF),
        vmem((side, half_side), BF),
        vmem((count, OUT_VARS, side), F32),
        vmem((count + 1, 8, side), F32),
        vmem((slots, OCEAN_CH, side), F32),
        vmem((slots, 1, side), F32),
        vmem((slots, 1, side), F32),
    ]
    for _ in range(5):
        scratch += [
            vmem((tiles, faces, 16, 2 * C), BF),
            vmem((2, faces, 16, 2 * C), BF),
            vmem((2 * faces, 16, 2 * C), BF),
            vmem((2 * groups * 2 * faces, 16, 2 * C), BF),
            vmem((2, faces, 16, 2 * C), BF),
            vmem((tiles, faces, 16, 2 * C), BF),
        ]
    scratch += [pltpu.SemaphoreType.DMA((5, SEM_COLS)), pltpu.SemaphoreType.DMA((5,))]
    smem = pl.BlockSpec(memory_space=pltpu.SMEM)
    whole = pl.BlockSpec(memory_space=pltpu.VMEM)
    out, sea = pl.pallas_call(
        functools.partial(kernel, groups, tiles, rows, faces),
        out_shape=(
            jax.ShapeDtypeStruct((count, OUT_VARS, side), F32),
            jax.ShapeDtypeStruct((slots, 1, side), F32),
        ),
        in_specs=[smem] * 3 + [pl.BlockSpec(memory_space=pl.ANY)] + [whole] * 10,
        out_specs=(whole, whole),
        scratch_shapes=scratch,
        compiler_params=pltpu.CompilerParams(
            collective_id=0, has_side_effects=True, vmem_limit_bytes=56 * 1024 * 1024
        ),
        name="coupled_step",
    )(
        seam_table, inverse, slot, atmos, land, held, w1, w2, w3, w4, w5, head, oin, oout
    )
    atmos_next = jnp.transpose(out.reshape(faces, rows, OUT_VARS, side), (2, 0, 1, 3)).astype(BF)
    ocean_next = jnp.concatenate([sea, held[:, :1]], axis=1)
    return atmos_next, ocean_next[None, None]


def solution(mesh):
    in_specs = (
        P(None, "face", "tile", None),
        P("face", "tile", None),
        P(("face", "tile"), None),
        P(),
        P("face", "tile", None, None, None),
        P(),
        P(),
        P(),
        P(),
        P(),
        P(),
        P(),
    )
    out_specs = (P(None, "face", "tile", None), P("face", "tile", None, None, None))
    return jax.shard_map(
        on_device, mesh=mesh, in_specs=in_specs, out_specs=out_specs, check_vma=False
    )
```

time: 469 us -> 168 us (0.36); the launches traced: 460 us -> 167 us
  Pallas kernels: 0 us -> 150 us
  local copies, waits for them, and re-layouts: 142 us -> 14.5 us
  starting transfers between devices: 102 us -> 0 us
  waiting for transfers between devices: 69.8 us -> 0 us
  other arithmetic: 58.2 us -> 2.24 us
  matrix products: 42.8 us -> 0 us
  blocking collectives: 41.5 us -> 0 us
    pallas_call x0 -> x1, Pallas kernels: none -> 150 us  [on_device(): pl.pallas_call(functools.partial(kernel, groups, tiles, rows, faces), out...]
    all_to_all x12 -> x0, starting transfers between devices: 68.7 us -> none  [the longest x5 32.1 us: sent_to_all(): return lax.all_to_all(copies, axis, split_axis=0, concat_axis=0, tiled=True)]
    all_to_all x12 -> x0, waiting for transfers between devices: 58.2 us -> none  [the longest x5 33.1 us: pad_field(): lax.all_to_all(edge_pieces, 'tile', split_axis=3, concat_axis=3, tiled=True)]
    concatenate x52 -> x0, local copies, waits for them, and re-layouts: 48.1 us -> none  [the longest x51 47.9 us: convolve(): jnp.concatenate([padded[:, face_index, row_shift:row_shift + stripe_rows,...]
    dot_general x103 -> x0, matrix products: 42.8 us -> none  [the longest x36 25.2 us: convolve(): jnp.dot(weight[row_shift], tap_rows.reshape(3 * channels, stripe_rows * f...]
    all_gather x5 -> x0, blocking collectives: 41.5 us -> none  [pad_field(): grouped = lax.all_gather(seam_piece, 'face', axis=0, tiled=True)]
    ppermute x10 -> x0, starting transfers between devices: 33.1 us -> none  [the longest x5 28.3 us: extended(): after = lax.ppermute(initial, axis, down)]
    squeeze x37 -> x0, local copies, waits for them, and re-layouts: 21.7 us -> none  [the longest x32 21.7 us: ocean_blocks(): lax.map(lambda pair: ocean_update(pair[0], pair[1], ocean_in, ocean_out),...]
  transfers between devices with their start and end apart: 22 -> 0, of which waited for: 11 -> 0; matrix products, arithmetic and copies ran while one was open for 23% -> 0% of each run, Pallas kernels for 0% -> 0%
where the time goes in v1:
time: 168 us; the launch traced here: 167 us
  Pallas kernels  150 us (89%)
  local copies, waits for them, and re-layouts  14.5 us (9%)
  other arithmetic  2.24 us (1%)
    pallas_call x1, Pallas kernels, on_device(): pl.pallas_call(functools.partial(kernel, groups, tiles, rows, faces), out...  150 us
    unnamed x33, local copies, waits for them, and re-layouts  4.23 us
    reshape x5, local copies, waits for them, and re-layouts, stacked_weight(): pieces.append(folded[..., at:at + C].reshape(3 * made, taps * C))  4.04 us

profile of v1, /device:TPU:1, one launch (start us, length us, event | category | flops | bytes accessed | tf_op | source)
XLA Modules:
  0.0 167.3 jit_solution(14884668111949420143)
XLA Ops:
  0.6 0.6 copy-done.12
  1.3 0.2 convert_reduce_fusion
  1.5 0.5 copy-done.9
  2.1 0.6 broadcast_add_fusion.inv_ref
  2.6 1.0 reshape.61
  3.6 0.2 fusion.1
  3.9 0.8 reshape.62.w4_ref
  4.9 0.8 reshape.63.w5_ref
  5.8 1.0 pad.12.clone
  7.3 0.8 reshape.56.w1_ref
  8.5 0.8 reshape.58.w2_ref
  9.5 0.2 copy.42
  9.7 0.8 reshape.60.w3_ref
  10.7 0.6 pad.14.oin_ref
  11.3 0.7 copy-done.11
  11.9 0.7 copy.47.oout_ref
  12.6 0.7 copy.46.seam_ref
  13.3 0.6 reshape.54.land_ref
  14.0 0.7 slice-done
  14.7 0.6 pad_maximum_fusion.head_ref
  15.3 149.7 %coupled_step.1 = (f32[24,8,256]{2,1,0:T(8,128)}, f32[64,1,256]{2,1,0:T(1,128)}) custom-call(s32[48,2]{1,0:T(8,128)} %copy.46.seam_ref, s32[64]{0:T(128)} %broadcast_add_fusion.inv_ref, s32[24]{0:T(128)} %copy-done.9, bf16[3,512,256]{2,1,0:T(8,128)(2,1)} %bitcast.22, s32[24,1,256]{2,1,0:T(1,128)} %reshape.54.land_ref, f32[64,2,256]{2,1,0:T(2,128)} %bitcast.29, ...), custom_call_target="tpu_custom_call" | custom-call | tf_op jit(solution)/shard_map/coupled_step/pallas_call | solution.py:603
  165.1 0.8 copy-done.5
  165.8 0.8 maximum_bitcast_fusion
  166.6 0.7 copy.52
  (40 shorter events, 1.8 us)
Async XLA Ops:
  0.6 0.7 copy-start.12
  1.5 0.5 copy-start.9
  4.8 1.0 copy-start
  5.8 1.0 copy-start.6
  7.3 0.9 copy-start.3
  8.5 0.9 copy-start.4
  9.7 0.8 copy-start.8
  11.3 0.7 copy-start.11
  11.9 0.7 copy-start.10
  11.9 1.4 copy-start.7
  14.0 0.7 slice-start
  14.0 0.7 slice-start.1
  15.3 149.8 %copy-start.1 = (f32[1,1,64,2,256]{4,3,2,1,0:T(2,128)S(1)}, f32[1,1,64,2,256]{4,3,2,1,0:T(2,128)}, u32[]{:S(2)}) copy-start(f32[1,1,64,2,256]{4,3,2,1,0:T(2,128)} %param.16) | copy-start | bytes 393220
  165.0 0.8 copy-start.5
  165.0 1.6 copy-start.2

commit v2 on v1

--- a/solution.py
+++ b/solution.py
@@ -18,8 +18,8 @@
 TN = (((0,), (0,)), ((), ()))
 
 HALO_SEND, HALO_UP, HALO_DOWN, SCAT_SEND, SCAT_TOP, SCAT_BOT = range(6)
-TAB_SEND, TAB_RECV, PICK_SEND, PICK_RECV, SEM_COLS = 6, 7, 8, 10, 12
-HALO_DOWN_SEND = 11
+TAB_SEND, TAB_RECV, PICK_SEND, PICK_RECV, HALO_DOWN_SEND = 6, 7, 8, 10, 11
+MIRROR_SEND, MIRROR_RECV, SEM_COLS = 12, 13, 14
 
 
 def iota(shape, dim):
@@ -33,7 +33,8 @@
 class Level:
     def __init__(self, rows, side, body, sems, bufs, sel):
         self.rows, self.side, self.body, self.sems = rows, side, body, sems
-        self.scat, self.scat_in, self.tab, self.tabs, self.pick, self.gath = bufs
+        self.scat, self.scat_in, self.tab, self.tabs, self.pick, self.gath = bufs[:6]
+        self.send, self.mirror = bufs[6:]
         self.sel = sel
 
 
@@ -52,7 +53,6 @@
     w2_ref,
     w3_ref,
     w4_ref,
-    w5_ref,
     head_ref,
     oin_ref,
     oout_ref,
@@ -73,6 +73,16 @@
     visit,
     sea_out,
     sea_in,
+    w1,
+    w2,
+    w3,
+    w4,
+    w5,
+    head,
+    oout,
+    before,
+    idle,
+    tile_sea,
     *rest,
 ):
     bufs, (sems, misc) = rest[:-2], rest[-2:]
@@ -98,35 +108,66 @@
             (half_rows, half_side, body4, sel_c),
         )
     ):
-        levels.append(Level(n, s, body, sems.at[number], bufs[6 * number : 6 * number + 6], sel))
-
-    for n, s, sel in ((rows, side, sel_f), (half_rows, half_side, sel_c)):
-        shape = (tiles * 16, s)
-        q, x = iota(shape, 0), iota(shape, 1)
-        k = q % 16
-        cell = (q // 16) * n + k - 1
-        inner = (k >= 1) & (k <= n)
-        sel[0] = jnp.where((x == cell) & (k <= n + 1), 1.0, 0.0).astype(BF)
-        sel[1] = jnp.where((x == cell) & inner, 1.0, 0.0).astype(BF)
-        sel[2] = jnp.where((x == s - 1 - cell) & inner, 1.0, 0.0).astype(BF)
+        levels.append(Level(n, s, body, sems.at[number], bufs[8 * number : 8 * number + 8], sel))
+
+    barrier = pltpu.get_barrier_semaphore()
+
+    def greet(d, carry):
+        peer = lax.rem(t + d, tiles)
+        pl.semaphore_signal(barrier, inc=1, device_id=(f, peer), device_id_type=MESH)
+        return carry
+
+    lax.fori_loop(1, tiles, greet, 0)
+    for d in range(1, groups):
+        g = lax.rem(f + d, groups)
+        pl.semaphore_signal(barrier, inc=1, device_id=(g, t), device_id_type=MESH)
+
+    @pl.when(is_top | is_bot)
+    def _():
+        for n, s, sel in ((rows, side, sel_f), (half_rows, half_side, sel_c)):
+            shape = (tiles * 16, s)
+            q, x = iota(shape, 0), iota(shape, 1)
+            k = q % 16
+            start = (q // 16) * n
+            sel[0] = jnp.where((x == start + k - 1) & (k <= n + 1), 1.0, 0.0).astype(BF)
+            for at, least in ((1, 0), (2, 8)):
+                cell = start + k - least
+                inner = (k >= least) & (k < least + n)
+                sel[at] = jnp.where((x == cell) & inner, 1.0, 0.0).astype(BF)
+                sel[at + 2] = jnp.where((x == s - 1 - cell) & inner, 1.0, 0.0).astype(BF)
+
     shape = (half_side, side)
     up_mat[...] = jnp.where(iota(shape, 1) // 2 == iota(shape, 0), 1.0, 0.0).astype(BF)
     shape = (side, half_side)
     down_mat[...] = jnp.where(iota(shape, 0) // 2 == iota(shape, 1), 0.25, 0.0).astype(BF)
 
-    barrier = pltpu.get_barrier_semaphore()
-
-    def greet(d, carry):
-        peer = lax.rem(t + d, tiles)
-        pl.semaphore_signal(barrier, inc=1, device_id=(f, peer), device_id_type=MESH)
-        return carry
-
-    lax.fori_loop(1, tiles, greet, 0)
-    for d in range(1, groups):
-        g = lax.rem(f + d, groups)
-        pl.semaphore_signal(barrier, inc=1, device_id=(g, t), device_id_type=MESH)
-        pl.semaphore_signal(barrier, inc=1, device_id=(g, last - t), device_id_type=MESH)
-    pl.semaphore_wait(barrier, tiles - 1 + 2 * (groups - 1))
+    for target, ref, first, width in (
+        (w1, w1_ref, 0, w1_ref.shape[2] // 3),
+        (w2, w2_ref, 0, C),
+        (w3, w3_ref, 0, C),
+        (w4, w4_ref, 0, C),
+        (w5, w4_ref, C, C),
+    ):
+        channels = ref.shape[2] // 3
+        for a in range(3):
+            whole = ref[a].astype(F32)
+            for b in range(3):
+                at = b * channels + first
+                block = whole[:, at : at + width]
+                if width < C:
+                    block = jnp.concatenate([block, jnp.zeros((C, C - width), F32)], axis=1)
+                target[pl.ds(b * C, C), pl.ds(a * C, C)] = block.astype(BF)
+    made = head_ref[...].astype(F32)
+    gap = jnp.zeros((2, C), F32)
+    head[...] = jnp.concatenate([made[:OUT_VARS], gap, made[OUT_VARS:], gap], axis=0).astype(BF)
+    diagonal = iota((C, C), 0) == iota((C, C), 1)
+    column = jnp.sum(
+        jnp.where(diagonal, jnp.broadcast_to(oout_ref[...], (C, C)), 0.0), axis=1, keepdims=True
+    )
+    oout[...] = jnp.broadcast_to(column, (C, side))
+
+    load.wait()
+    pl.semaphore_wait(barrier, tiles - 1 + groups - 1)
 
     def remote(src, dst, send, recv, device):
         return pltpu.make_async_remote_copy(
@@ -213,16 +254,13 @@
             drain(lv.scat_in.at[1], lv.sems.at[SCAT_BOT])
 
     def table_copy(lv, d):
-        mirrored = d // groups
-        g = lax.rem(f + d % groups, groups)
-        peer = last - t if mirrored else t
         width = 2 * faces
         return remote(
             lv.tab,
-            lv.tabs.at[pl.ds((mirrored * groups + f) * width, width)],
+            lv.tabs.at[pl.ds(f * width, width)],
             lv.sems.at[TAB_SEND],
             lv.sems.at[TAB_RECV],
-            (g, peer),
+            (lax.rem(f + d, groups), t),
         )
 
     def begin_tables(lv):
@@ -247,31 +285,46 @@
             return carry
 
         lax.fori_loop(0, faces, one_face, 0)
-        for d in range(1, 2 * groups):
+        for d in range(1, groups):
             table_copy(lv, d).start()
         lv.tabs[pl.ds(f * 2 * faces, 2 * faces)] = lv.tab[...]
 
     def end_tables(lv):
-        drain(lv.tabs.at[pl.ds(0, (2 * groups - 1) * 2 * faces)], lv.sems.at[TAB_RECV])
+        drain(lv.tabs.at[pl.ds(0, (groups - 1) * 2 * faces)], lv.sems.at[TAB_RECV])
 
     def row_copy(lv, which):
         return remote(
-            lv.pick.at[which],
+            lv.send.at[which],
             lv.gath.at[t],
             lv.sems.at[PICK_SEND + which],
             lv.sems.at[PICK_RECV],
             (f, 0 if which == 0 else last),
         )
 
+    def mirror_copy(lv):
+        return remote(
+            lv.pick, lv.mirror, lv.sems.at[MIRROR_SEND], lv.sems.at[MIRROR_RECV], (f, last - t)
+        )
+
     def seam(j, s):
         at = (f * faces + j) * 4 + s
-        return seam_ref[at, 0], seam_ref[at, 1]
+        return seam_ref[0, at], seam_ref[1, at]
 
     def begin_strips(lv):
+        n = lv.rows
+        shape = (16, 16)
+        r, k = iota(shape, 0), iota(shape, 1)
+        low = jnp.where((k == r + 1) & (r < n), 1.0, 0.0).astype(BF)
+        high = jnp.where((k == r - 7) & (r >= 8) & (r < 8 + n), 1.0, 0.0).astype(BF)
         for which, cond in ((0, is_top), (1, is_bot)):
+            parts = []
             for j in range(faces):
                 p, _ = seam(j, which)
-                lv.pick[which, j] = lv.tabs[p // 2]
+                spread = jnp.dot(
+                    high if j == 2 else low, lv.tabs[p // 2], preferred_element_type=F32
+                )
+                parts.append(jnp.where(p % 2 == 1, spread[:, C:], spread[:, :C]))
+            lv.send[which] = jnp.concatenate([parts[0] + parts[2], parts[1]], axis=1).astype(BF)
 
             @pl.when(jnp.logical_not(cond))
             def _(which=which):
@@ -279,7 +332,13 @@
 
             @pl.when(cond)
             def _(which=which):
-                lv.gath[0 if which == 0 else last] = lv.pick[which]
+                lv.gath[0 if which == 0 else last] = lv.send[which]
+
+        for s in (2, 3):
+            for j in range(faces):
+                p, _ = seam(j, s)
+                lv.pick[s - 2, j] = lv.tabs[p // 2]
+        mirror_copy(lv).start()
 
     def column_strips(lv, j, store):
         n = lv.rows
@@ -288,7 +347,7 @@
         total = jnp.zeros((C, 128), F32)
         for s in (2, 3):
             p, rev = seam(j, s)
-            piece = lv.tabs[rev * (groups * 2 * faces) + p // 2]
+            piece = jnp.where(rev == 1, lv.mirror[s - 2, j], lv.pick[s - 2, j])
             kk = jnp.where(rev == 1, n + 1 - k, k)
             good = (kk >= jnp.where(is_top, 1, 0)) & (kk <= jnp.where(is_bot, n, n + 1))
             want = (2 * kk + 127) % 128 if s == 2 else 2 * kk
@@ -297,7 +356,12 @@
             total += jnp.where(p % 2 == 1, both[C:], both[:C])
         store(j, total)
 
+    def end_mirror(lv):
+        drain(lv.mirror, lv.sems.at[MIRROR_RECV])
+
     def store_columns(lv):
+        end_mirror(lv)
+
         def store(j, total):
             for k in range(lv.rows + 2):
                 lv.body[j, pl.ds(k * C, C), pl.ds(lv.side, 128)] = pltpu.roll(
@@ -318,12 +382,11 @@
             def _(which=which):
                 drain(lv.gath.at[pl.ds(0, tiles - 1)], lv.sems.at[PICK_RECV])
                 for j in range(faces):
-                    p, rev = seam(j, which)
-                    pieces = lv.gath[:, j].reshape(tiles * 16, 2 * C)
-                    both = lax.dot_general(
-                        pieces, lv.sel[1 + rev], TN, preferred_element_type=F32
-                    )
-                    strip = jnp.where(p % 2 == 1, both[C:], both[:C])
+                    _, rev = seam(j, which)
+                    pieces = lv.gath[...].reshape(tiles * 16, 2 * C)
+                    chosen = lv.sel[(2 if j == 2 else 1) + 2 * rev]
+                    both = lax.dot_general(pieces, chosen, TN, preferred_element_type=F32)
+                    strip = both[C:] if j == 1 else both[:C]
                     at = 0 if which == 0 else (n + 1) * C
                     lv.body[j, pl.ds(at, C), pl.ds(0, s)] = strip.astype(BF)
 
@@ -344,7 +407,8 @@
         def _():
             drain(lv.scat.at[pl.ds(0, tiles - 1)], lv.sems.at[SCAT_SEND])
 
-        drain(lv.tabs.at[pl.ds(0, (2 * groups - 1) * 2 * faces)], lv.sems.at[TAB_SEND])
+        drain(lv.tabs.at[pl.ds(0, (groups - 1) * 2 * faces)], lv.sems.at[TAB_SEND])
+        mirror_copy(lv).wait_send()
 
     def taps(product, s):
         wide = s + 128
@@ -394,7 +458,6 @@
         lax.fori_loop(1, tiles, body, 0)
 
     lv1, lv2, lv3, lvs, lv4 = levels
-    load.wait()
     begin_rows(lv1)
     start_all(state_copy)
     visit[pl.ds(2 * t, 2)] = held_ref[pl.ds(2 * t, 2)]
@@ -405,16 +468,32 @@
         end_tables(lv)
         begin_strips(lv)
 
+    def early_ocean():
+        drain(visit.at[pl.ds(0, 2 * (tiles - 1))], misc.at[2])
+        w_a = jnp.broadcast_to(oin_ref[:, 0:1], (C, side))
+        w_b = jnp.broadcast_to(oin_ref[:, 1:2], (C, side))
+
+        def one_slot(n, carry):
+            old = visit[n]
+            total = w_a * old[:1] + w_b * old[1:]
+            before[n] = total
+            moved = jnp.sum(oout[...] * jax.nn.gelu(total), axis=0, keepdims=True)
+            idle[n] = old[:1] + moved
+            return carry
+
+        lax.fori_loop(0, 2 * tiles, one_slot, 0)
+
     exchange(lv1)
+    early_ocean()
     store_columns(lv1)
     end_strips(lv1)
-    conv(lv1, w1_ref, body2)
+    conv(lv1, w1, body2)
 
     begin_rows(lv2)
     exchange(lv2)
     store_columns(lv2)
     end_strips(lv2)
-    conv(lv2, w2_ref, bodys)
+    conv(lv2, w2, bodys)
 
     def pool(i, carry):
         j, q = i // half_rows, i % half_rows
@@ -431,7 +510,7 @@
     exchange(lv3)
     store_columns(lv3)
     end_strips(lv3)
-    conv(lv3, w3_ref, body4)
+    conv(lv3, w3, body4)
 
     begin_rows(lv4)
     exchange(lvs)
@@ -449,6 +528,7 @@
         column_strips(lv4, j, store_coarse)
         return carry
 
+    end_mirror(lv4)
     lax.fori_loop(0, faces, coarse_columns, 0)
     end_strips(lv4)
 
@@ -467,43 +547,52 @@
     def decode(i, carry):
         j, r = i // rows, i % rows
         window = pl.ds(pl.multiple_of(r * C, C), 3 * C)
-        product = jnp.dot(w4_ref[...], bodys[j, window, :], preferred_element_type=F32)
-        product += jnp.dot(w5_ref[...], bodyc[j, window, :], preferred_element_type=F32)
+        product = jnp.dot(w4[...], bodys[j, window, :], preferred_element_type=F32)
+        product += jnp.dot(w5[...], bodyc[j, window, :], preferred_element_type=F32)
         decoded = jax.nn.gelu(taps(product, side)).astype(BF)
-        head = jnp.dot(head_ref[...], decoded, preferred_element_type=F32)
+        out = jnp.dot(head[...], decoded, preferred_element_type=F32)
         state = body1[j, pl.ds(pl.multiple_of(r * C + C, C), 16), pl.ds(0, side)]
-        pred[i] = state[:OUT_VARS].astype(F32) + head[:OUT_VARS]
-        ocean = jnp.broadcast_to(land_ref[i] == 1, (8, side))
-        flux[i] = jnp.where(ocean, head[OUT_VARS:], 0.0).astype(BF).astype(F32)
+        pred[i] = state[:OUT_VARS].astype(F32) + out[:OUT_VARS]
+        wet = jnp.broadcast_to(land_ref[j, pl.ds(r, 1), :] == 1, (8, side))
+        flux[i] = jnp.where(wet, out[OUT_VARS:], 0.0).astype(BF)
         return carry
 
     lax.fori_loop(0, faces * rows, decode, 0)
-    flux[faces * rows] = jnp.zeros((8, side), F32)
-
-    drain(visit.at[pl.ds(0, 2 * (tiles - 1))], misc.at[2])
-
-    def ocean(n, carry):
-        old = visit[n]
-        stacked = jnp.concatenate([old, jnp.zeros((6, side), F32)], axis=0) + flux[inv_ref[n]]
+
+    flux_in = jnp.concatenate(
+        [jnp.zeros((C, 2), F32), oin_ref[:, OCEAN_CH:], jnp.zeros((C, 2), F32)], axis=1
+    )
+    first = flux_in.astype(BF)
+    second = (flux_in - first.astype(F32)).astype(BF)
+    third = (flux_in - first.astype(F32) - second.astype(F32)).astype(BF)
+    split = jnp.concatenate([first, second, third], axis=0)
+
+    def ocean(i, carry):
+        slot = slot_ref[i]
+        parts = jnp.dot(split, flux[i], preferred_element_type=F32)
         hidden = jax.nn.gelu(
-            jnp.dot(
-                oin_ref[...],
-                stacked,
-                preferred_element_type=F32,
-                precision=lax.Precision.HIGHEST,
-            )
-        )
-        moved = jnp.sum(oout_ref[...] * hidden, axis=0, keepdims=True)
-        sea_out[n] = old[:1] + moved
+            before[slot] + (parts[:C] + (parts[C : 2 * C] + parts[2 * C :]))
+        )
+        moved = jnp.sum(oout[...] * hidden, axis=0, keepdims=True)
+        tile_sea[i] = visit[slot][:1] + moved
         return carry
 
-    lax.fori_loop(0, 2 * tiles, ocean, 0)
+    lax.fori_loop(0, faces * rows, ocean, 0)
+
+    def fill(n, carry):
+        tile = inv_ref[n]
+        used = tile < faces * rows
+        sea_out[n] = jnp.where(used, tile_sea[jnp.where(used, tile, 0)], idle[n])
+        return carry
+
+    lax.fori_loop(0, 2 * tiles, fill, 0)
     start_all(sea_copy)
     sea_in[pl.ds(2 * t, 2)] = sea_out[pl.ds(2 * t, 2)]
 
     def surface(i, carry):
-        sea = jnp.broadcast_to(sea_out[slot_ref[i]], (8, side))
-        wet = jnp.broadcast_to(land_ref[i] == 1, (8, side)) & (iota((8, side), 0) == 0)
+        sea = jnp.broadcast_to(tile_sea[i], (8, side))
+        wet = jnp.broadcast_to(land_ref[i // rows, pl.ds(i % rows, 1), :] == 1, (8, side))
+        wet = wet & (iota((8, side), 0) == 0)
         out_ref[i] = jnp.where(wet, sea, pred[i])
         return carry
 
@@ -515,18 +604,6 @@
         finish_sends(lv)
     drain(held_ref.at[pl.ds(0, 2 * (tiles - 1))], misc.at[1])
     drain(sea_out.at[pl.ds(0, 2 * (tiles - 1))], misc.at[3])
-
-
-def stacked_weight(weight):
-    taps, made, wide = weight.shape
-    channels = wide // 3
-    folded = jnp.transpose(weight.reshape(taps, made, 3, channels), (2, 1, 0, 3))
-    if channels < C:
-        folded = jnp.pad(folded, ((0, 0), (0, 0), (0, 0), (0, C - channels)))
-    pieces = []
-    for at in range(0, folded.shape[3], C):
-        pieces.append(folded[..., at : at + C].reshape(3 * made, taps * C))
-    return pieces
 
 
 def on_device(
@@ -549,7 +626,6 @@
     slots = ocean_state.shape[2]
     atmos = jnp.pad(jnp.transpose(atmos_state, (1, 2, 0, 3)), ((0, 0), (0, 0), (0, C - channels), (0, 0)))
     atmos = atmos.reshape(faces, rows * C, side)
-    land = land_sea.reshape(count, 1, side)
     owner_ids = owners[:, 0]
     same = owner_ids[:, None] == owner_ids[None, :]
     earlier = jnp.arange(count)[None, :] < jnp.arange(count)[:, None]
@@ -560,15 +636,6 @@
         jnp.where(hits, jnp.arange(count)[None, :] - count, 0), axis=1
     )
     held = ocean_state[0, 0]
-    (w1,) = stacked_weight(conv_input)
-    (w2,) = stacked_weight(conv_encode)
-    (w3,) = stacked_weight(conv_coarse)
-    w4, w5 = stacked_weight(conv_decode)
-    gap = jnp.zeros((OCEAN_CH, output_head.shape[1]), output_head.dtype)
-    head = jnp.concatenate([output_head[:OUT_VARS], gap, output_head[OUT_VARS:], gap], axis=0)
-    oin = jnp.pad(ocean_in, ((0, 0), (0, 8 - ocean_in.shape[1])))
-    oout = ocean_out[:, None]
-
     half_rows, half_side = rows // 2, side // 2
     vmem = pltpu.VMEM
     scratch = [
@@ -578,24 +645,34 @@
         vmem((faces, (rows + 2) * C, side + 128), BF),
         vmem((faces, (half_rows + 2) * C, half_side), BF),
         vmem((faces, (rows + 2) * C, side + 128), BF),
-        vmem((3, tiles * 16, side), BF),
-        vmem((3, tiles * 16, half_side), BF),
+        vmem((5, tiles * 16, side), BF),
+        vmem((5, tiles * 16, half_side), BF),
         vmem((half_side, side), BF),
         vmem((side, half_side), BF),
         vmem((count, OUT_VARS, side), F32),
-        vmem((count + 1, 8, side), F32),
+        vmem((count, 8, side), BF),
         vmem((slots, OCEAN_CH, side), F32),
         vmem((slots, 1, side), F32),
         vmem((slots, 1, side), F32),
+    ]
+    scratch += [vmem((3 * C, 3 * C), BF)] * 5
+    scratch += [
+        vmem((16, C), BF),
+        vmem((C, side), F32),
+        vmem((slots, C, side), F32),
+        vmem((slots, 1, side), F32),
+        vmem((count, 1, side), F32),
     ]
     for _ in range(5):
         scratch += [
             vmem((tiles, faces, 16, 2 * C), BF),
             vmem((2, faces, 16, 2 * C), BF),
             vmem((2 * faces, 16, 2 * C), BF),
-            vmem((2 * groups * 2 * faces, 16, 2 * C), BF),
+            vmem((groups * 2 * faces, 16, 2 * C), BF),
             vmem((2, faces, 16, 2 * C), BF),
-            vmem((tiles, faces, 16, 2 * C), BF),
+            vmem((tiles, 16, 2 * C), BF),
+            vmem((2, 16, 2 * C), BF),
+            vmem((2, faces, 16, 2 * C), BF),
         ]
     scratch += [pltpu.SemaphoreType.DMA((5, SEM_COLS)), pltpu.SemaphoreType.DMA((5,))]
     smem = pl.BlockSpec(memory_space=pltpu.SMEM)
@@ -606,7 +683,7 @@
             jax.ShapeDtypeStruct((count, OUT_VARS, side), F32),
             jax.ShapeDtypeStruct((slots, 1, side), F32),
         ),
-        in_specs=[smem] * 3 + [pl.BlockSpec(memory_space=pl.ANY)] + [whole] * 10,
+        in_specs=[smem] * 3 + [pl.BlockSpec(memory_space=pl.ANY)] + [whole] * 9,
         out_specs=(whole, whole),
         scratch_shapes=scratch,
         compiler_params=pltpu.CompilerParams(
@@ -614,7 +691,19 @@
         ),
         name="coupled_step",
     )(
-        seam_table, inverse, slot, atmos, land, held, w1, w2, w3, w4, w5, head, oin, oout
+        seam_table.T,
+        inverse,
+        slot,
+        atmos,
+        land_sea,
+        held,
+        conv_input,
+        conv_encode,
+        conv_coarse,
+        conv_decode,
+        output_head,
+        ocean_in,
+        ocean_out[None],
     )
     atmos_next = jnp.transpose(out.reshape(faces, rows, OUT_VARS, side), (2, 0, 1, 3)).astype(BF)
     ocean_next = jnp.concatenate([sea, held[:, :1]], axis=1)

time: 168 us -> 141 us (0.84)
  Pallas kernels: 150 us -> 133 us
  local copies, waits for them, and re-layouts: 14.5 us -> 5.46 us
    pallas_call x1, Pallas kernels: 150 us -> 133 us  [on_device(): pl.pallas_call(functools.partial(kernel, groups, tiles, rows, faces), out...]
    reshape x7 -> x0, local copies, waits for them, and re-layouts: 5.63 us -> none  [the longest x5 4.04 us: stacked_weight(): pieces.append(folded[..., at:at + C].reshape(3 * made, taps * C))]
    unnamed x33 -> x14, local copies, waits for them, and re-layouts: 4.23 us -> 3.77 us
where the time goes in v2:
time: 141 us; the launch traced here: 140 us
  Pallas kernels  133 us (94%)
  local copies, waits for them, and re-layouts  5.46 us (4%)
  other arithmetic  1.58 us (1%)
    pallas_call x1, Pallas kernels, on_device(): pl.pallas_call(functools.partial(kernel, groups, tiles, rows, faces), out...  133 us
    unnamed x14, local copies, waits for them, and re-layouts  3.77 us

profile of v2, /device:TPU:1, one launch (start us, length us, event | category | flops | bytes accessed | tf_op | source)
XLA Modules:
  0.0 140.4 jit_solution(8801180443405168091)
XLA Ops:
  0.6 0.0 copy-start.5
  0.6 0.6 copy-done.5
  1.3 0.2 convert_reduce_fusion
  1.5 0.0 copy-start.4
  1.5 0.6 copy-done.4
  2.1 0.1 select_reduce_fusion
  2.1 0.5 broadcast_add_fusion.inv_ref
  2.7 1.1 copy.20
  3.7 0.0 copy-start.3
  3.7 1.0 pad.4.clone
  4.7 0.0 copy-done.3
  4.7 0.7 copy.18.oin_ref
  5.4 0.0 copy-start
  5.4 132.6 %coupled_step.1 = (f32[24,8,256]{2,1,0:T(8,128)}, f32[64,1,256]{2,1,0:T(1,128)}) custom-call(s32[2,48]{1,0:T(2,128)} %bitcast.19, s32[64]{0:T(128)} %broadcast_add_fusion.inv_ref, s32[24]{0:T(128)} %copy-done.4, bf16[3,512,256]{2,1,0:T(8,128)(2,1)} %bitcast.13, s32[3,8,256]{2,1,0:T(8,128)} %land_ref.1, f32[64,2,256]{2,1,0:T(2,128)} %bitcast.16, ...), custom_call_target="tpu_custom_call" | custom-call | tf_op jit(solution)/shard_map/coupled_step/pallas_call | solution.py:680
  138.1 0.0 copy-start.2
  138.1 0.0 copy-done
  138.1 0.0 copy-start.1
  138.2 0.8 copy-done.2
  138.9 0.8 maximum_bitcast_fusion
  139.7 0.0 copy-done.1
  139.7 0.7 copy.22
  (3 shorter events, 0.1 us)
Async XLA Ops:
  0.6 0.7 copy-start.5
  1.5 0.6 copy-start.4
  3.7 1.0 copy-start.3
  5.4 132.6 %copy-start = (f32[1,1,64,2,256]{4,3,2,1,0:T(2,128)S(1)}, f32[1,1,64,2,256]{4,3,2,1,0:T(2,128)}, u32[]{:S(2)}) copy-start(f32[1,1,64,2,256]{4,3,2,1,0:T(2,128)} %param.16) | copy-start | bytes 393220
  138.1 0.8 copy-start.2
  138.1 1.6 %copy-start.1 = (f32[24,8,256]{2,1,0:T(8,128)S(1)}, f32[24,8,256]{2,1,0:T(8,128)}, u32[]{:S(2)}) copy-start(f32[24,8,256]{2,1,0:T(8,128)} %get-tuple-element.4) | copy-start | bytes 589828

commit v3 on v2

--- a/solution.py
+++ b/solution.py
@@ -26,12 +26,19 @@
     return lax.broadcasted_iota(jnp.int32, shape, dim)
 
 
+def gelu(x):
+    inner = x * (0.7978845608028654 + 0.035677408136300125 * (x * x))
+    half = 0.5 * x
+    return half + half * jnp.tanh(inner)
+
+
 def drain(ref, sem):
     pltpu.make_async_copy(ref, ref, sem).wait()
 
 
 class Level:
-    def __init__(self, rows, side, body, sems, bufs, sel):
+    def __init__(self, rows, side, body, sems, bufs, sel, edge, strip):
+        self.edge, self.strip = edge, strip
         self.rows, self.side, self.body, self.sems = rows, side, body, sems
         self.scat, self.scat_in, self.tab, self.tabs, self.pick, self.gath = bufs[:6]
         self.send, self.mirror = bufs[6:]
@@ -83,6 +90,15 @@
     before,
     idle,
     tile_sea,
+    a1,
+    a2,
+    a3,
+    a4,
+    a5,
+    edges,
+    strips,
+    edgec,
+    made_edge,
     *rest,
 ):
     bufs, (sems, misc) = rest[:-2], rest[-2:]
@@ -108,7 +124,10 @@
             (half_rows, half_side, body4, sel_c),
         )
     ):
-        levels.append(Level(n, s, body, sems.at[number], bufs[8 * number : 8 * number + 8], sel))
+        own = bufs[8 * number : 8 * number + 8]
+        levels.append(
+            Level(n, s, body, sems.at[number], own, sel, edges.at[number], strips.at[number])
+        )
 
     barrier = pltpu.get_barrier_semaphore()
 
@@ -141,12 +160,12 @@
     shape = (side, half_side)
     down_mat[...] = jnp.where(iota(shape, 0) // 2 == iota(shape, 1), 0.25, 0.0).astype(BF)
 
-    for target, ref, first, width in (
-        (w1, w1_ref, 0, w1_ref.shape[2] // 3),
-        (w2, w2_ref, 0, C),
-        (w3, w3_ref, 0, C),
-        (w4, w4_ref, 0, C),
-        (w5, w4_ref, C, C),
+    for target, along, ref, first, width in (
+        (w1, a1, w1_ref, 0, w1_ref.shape[2] // 3),
+        (w2, a2, w2_ref, 0, C),
+        (w3, a3, w3_ref, 0, C),
+        (w4, a4, w4_ref, 0, C),
+        (w5, a5, w4_ref, C, C),
     ):
         channels = ref.shape[2] // 3
         for a in range(3):
@@ -157,6 +176,7 @@
                 if width < C:
                     block = jnp.concatenate([block, jnp.zeros((C, C - width), F32)], axis=1)
                 target[pl.ds(b * C, C), pl.ds(a * C, C)] = block.astype(BF)
+                along[pl.ds(a * C, C), pl.ds(b * C, C)] = block.astype(BF)
     made = head_ref[...].astype(F32)
     gap = jnp.zeros((2, C), F32)
     head[...] = jnp.concatenate([made[:OUT_VARS], gap, made[OUT_VARS:], gap], axis=0).astype(BF)
@@ -263,23 +283,43 @@
             (lax.rem(f + d, groups), t),
         )
 
+    lane = iota((C, 128), 1)
+
+    def widened(data, right):
+        missing = 128 - data.shape[1]
+        if missing <= 0:
+            return data
+        zero = jnp.zeros((C, missing), data.dtype)
+        return jnp.concatenate([zero, data] if right else [data, zero], axis=1)
+
+    def extract(body, edge, s, j, ks, fresh, clear):
+        total = jnp.zeros((C, 128), F32) if fresh else edge[j]
+        wide = min(s, 128)
+        for k in ks:
+            here = pl.ds(k * C, C)
+            left = widened(body[j, here, pl.ds(0, wide)].astype(F32), False)
+            right = widened(body[j, here, pl.ds(s - wide, wide)].astype(F32), True)
+            if clear and k == 0:
+                left, right = (jnp.where(is_top, 0.0, v) for v in (left, right))
+            if clear and k == ks[-1]:
+                left, right = (jnp.where(is_bot, 0.0, v) for v in (left, right))
+            total = jnp.where(lane // 2 == k, pltpu.roll(left, 2 * k, 1), total)
+            total = jnp.where(
+                lane // 2 == 32 + k, pltpu.roll(right, (66 + 2 * k) % 128, 1), total
+            )
+        edge[j] = total
+        return total
+
     def begin_tables(lv):
         n, s = lv.rows, lv.side
-        shape = (32, s)
-        row, lane = iota(shape, 0), iota(shape, 1)
+        shape = (32, 128)
+        row, at = iota(shape, 0), iota(shape, 1)
+        want = jnp.where(row < 16, 2 * row, 64 + 2 * (row - 16) + 1)
+        pick = jnp.where((at == want) & (row % 16 < n + 2), 1.0, 0.0).astype(BF)
 
         def one_face(j, carry):
-            total = jnp.zeros((32, C), F32)
-            for k in range(n + 2):
-                pick = ((row == k) & (lane == 0)) | ((row == 16 + k) & (lane == s - 1))
-                data = lv.body[j, pl.ds(k * C, C), pl.ds(0, s)]
-                if k == 0:
-                    data = jnp.where(is_top, jnp.zeros_like(data), data)
-                if k == n + 1:
-                    data = jnp.where(is_bot, jnp.zeros_like(data), data)
-                total += lax.dot_general(
-                    jnp.where(pick, 1.0, 0.0).astype(BF), data, NT, preferred_element_type=F32
-                )
+            edge = extract(lv.body, lv.edge, s, j, range(n + 2), True, True)
+            total = lax.dot_general(pick, edge.astype(BF), NT, preferred_element_type=F32)
             lv.tab[2 * j + 1] = jnp.concatenate([total[:16], total[16:]], axis=1).astype(BF)
             lv.tab[2 * j] = lv.scat_in[0, j] + lv.scat_in[1, j]
             return carry
@@ -340,36 +380,72 @@
                 lv.pick[s - 2, j] = lv.tabs[p // 2]
         mirror_copy(lv).start()
 
-    def column_strips(lv, j, store):
+    def column_strips(lv, fine):
         n = lv.rows
         shape = (16, 128)
-        k, lane = iota(shape, 0), iota(shape, 1)
-        total = jnp.zeros((C, 128), F32)
-        for s in (2, 3):
-            p, rev = seam(j, s)
-            piece = jnp.where(rev == 1, lv.mirror[s - 2, j], lv.pick[s - 2, j])
-            kk = jnp.where(rev == 1, n + 1 - k, k)
-            good = (kk >= jnp.where(is_top, 1, 0)) & (kk <= jnp.where(is_bot, n, n + 1))
-            want = (2 * kk + 127) % 128 if s == 2 else 2 * kk
-            chosen = jnp.where(good & (lane == want), 1.0, 0.0).astype(BF)
-            both = lax.dot_general(piece, chosen, TN, preferred_element_type=F32)
-            total += jnp.where(p % 2 == 1, both[C:], both[:C])
-        store(j, total)
+        k, at = iota(shape, 0), iota(shape, 1)
+
+        def one_face(j, carry):
+            total = jnp.zeros((C, 128), F32)
+            for s in (2, 3):
+                p, rev = seam(j, s)
+                piece = jnp.where(rev == 1, lv.mirror[s - 2, j], lv.pick[s - 2, j])
+                kk = jnp.where(rev == 1, n + 1 - k, k)
+                good = (kk >= jnp.where(is_top, 1, 0)) & (kk <= jnp.where(is_bot, n, n + 1))
+                spot = at if s == 2 else at - 65
+                index = (spot // 2 + 1) // 2 if fine else spot // 2
+                good = good & (index == kk) & (spot % 2 == 0)
+                good = good & ((at < 64) if s == 2 else (at > 64))
+                chosen = jnp.where(good, 1.0, 0.0).astype(BF)
+                both = lax.dot_general(piece, chosen, TN, preferred_element_type=F32)
+                total += jnp.where(p % 2 == 1, both[C:], both[:C])
+            lv.strip[j] = total
+            return carry
+
+        lax.fori_loop(0, faces, one_face, 0)
 
     def end_mirror(lv):
         drain(lv.mirror, lv.sems.at[MIRROR_RECV])
 
-    def store_columns(lv):
-        end_mirror(lv)
-
-        def store(j, total):
-            for k in range(lv.rows + 2):
-                lv.body[j, pl.ds(k * C, C), pl.ds(lv.side, 128)] = pltpu.roll(
-                    total, (128 - 2 * k) % 128, 1
-                ).astype(BF)
-
+    def edge_terms(along, edge, strip):
+        near = jnp.where(lane < 64, strip, pltpu.roll(edge, 1, 1))
+        far = jnp.where(lane < 64, pltpu.roll(edge, 127, 1), strip)
+        stack = jnp.concatenate([near, edge, far], axis=0).astype(BF)
+        return jnp.dot(along[...], stack, preferred_element_type=F32)
+
+    def edge_sum(terms):
+        return (
+            terms[:C]
+            + pltpu.roll(terms[C : 2 * C], 126, 1)
+            + pltpu.roll(terms[2 * C :], 124, 1)
+        )
+
+    def make_edges(lv, along):
         def one_face(j, carry):
-            column_strips(lv, j, store)
+            made_edge[j] = gelu(edge_sum(edge_terms(along, lv.edge[j], lv.strip[j])))
+            return carry
+
+        lax.fori_loop(0, faces, one_face, 0)
+
+    def patch(s, r, values):
+        wide = min(s, 128)
+        spot = iota((values.shape[0], wide), 1)
+        low = pltpu.roll(values, (128 - 2 * r) % 128, 1)[:, :wide]
+        high = pltpu.roll(values, (2 * 128 + wide - 1 - 65 - 2 * r) % 128, 1)[:, :wide]
+        return low, high, spot == 0, spot == wide - 1, pl.ds(0, wide), pl.ds(s - wide, wide)
+
+    def fix(lv, target, r_list):
+        n, s = lv.rows, lv.side
+
+        def one_face(j, carry):
+            values = made_edge[j]
+            for r in r_list:
+                low, high, is_low, is_high, left, right = patch(s, r, values)
+                here = pl.ds((r + 1) * C, C)
+                old = target[j, here, left].astype(F32)
+                target[j, here, left] = jnp.where(is_low, low, old).astype(BF)
+                old = target[j, here, right].astype(F32)
+                target[j, here, right] = jnp.where(is_high, high, old).astype(BF)
             return carry
 
         lax.fori_loop(0, faces, one_face, 0)
@@ -411,24 +487,50 @@
         mirror_copy(lv).wait_send()
 
     def taps(product, s):
-        wide = s + 128
-        mid = product[C : 2 * C, :s]
-        left = pltpu.roll(product[:C], 1, 1)[:, :s]
-        right = pltpu.roll(product[2 * C :], wide - 1, 1)[:, :s]
-        return mid + left + right
-
-    def conv(lv, w_ref, target):
+        left = pltpu.roll(product[:C], 1, 1)
+        right = pltpu.roll(product[2 * C :], s - 1, 1)
+        return product[C : 2 * C] + left + right
+
+    def conv_row(lv, w, target, j, r):
         n, s = lv.rows, lv.side
-
-        def one_row(i, carry):
-            j, r = i // n, i % n
-            window = lv.body[j, pl.ds(pl.multiple_of(r * C, C), 3 * C), :]
-            product = jnp.dot(w_ref[...], window, preferred_element_type=F32)
-            made = jax.nn.gelu(taps(product, s)).astype(BF)
-            target[j, pl.ds(pl.multiple_of(r * C + C, C), C), pl.ds(0, s)] = made
+        window = lv.body[j, pl.ds(pl.multiple_of(r * C, C), 3 * C), :]
+        product = jnp.dot(w[...], window, preferred_element_type=F32)
+        made = gelu(taps(product, s)).astype(BF)
+        target[j, pl.ds(pl.multiple_of(r * C + C, C), C), :] = made
+
+    def inner_rows(n, one_row):
+        def body(i, carry):
+            one_row(i // (n - 2), 1 + i % (n - 2))
             return carry
 
-        lax.fori_loop(0, faces * n, one_row, 0)
+        lax.fori_loop(0, faces * (n - 2), body, 0)
+
+    def outer_rows(n, one_row):
+        def body(j, carry):
+            @pl.when(jnp.logical_not(is_top))
+            def _():
+                one_row(j, 0)
+
+            @pl.when(jnp.logical_not(is_bot))
+            def _():
+                one_row(j, n - 1)
+
+            return carry
+
+        lax.fori_loop(0, faces, body, 0)
+
+    def end_row(lv, one_row):
+        n = lv.rows
+        for cond, k, r in ((is_top, 0, 0), (is_bot, n + 1, n - 1)):
+
+            @pl.when(cond)
+            def _(k=k, r=r):
+                def body(j, carry):
+                    extract(lv.body, lv.edge, lv.side, j, (k,), False, False)
+                    one_row(j, r)
+                    return carry
+
+                lax.fori_loop(0, faces, body, 0)
 
     def state_copy(d):
         dst = lax.rem(t + d, tiles)
@@ -462,12 +564,6 @@
     start_all(state_copy)
     visit[pl.ds(2 * t, 2)] = held_ref[pl.ds(2 * t, 2)]
 
-    def exchange(lv):
-        end_rows(lv)
-        begin_tables(lv)
-        end_tables(lv)
-        begin_strips(lv)
-
     def early_ocean():
         drain(visit.at[pl.ds(0, 2 * (tiles - 1))], misc.at[2])
         w_a = jnp.broadcast_to(oin_ref[:, 0:1], (C, side))
@@ -477,87 +573,148 @@
             old = visit[n]
             total = w_a * old[:1] + w_b * old[1:]
             before[n] = total
-            moved = jnp.sum(oout[...] * jax.nn.gelu(total), axis=0, keepdims=True)
+            moved = jnp.sum(oout[...] * gelu(total), axis=0, keepdims=True)
             idle[n] = old[:1] + moved
             return carry
 
         lax.fori_loop(0, 2 * tiles, one_slot, 0)
 
-    exchange(lv1)
-    early_ocean()
-    store_columns(lv1)
-    end_strips(lv1)
-    conv(lv1, w1, body2)
-
+    def level(lv, w, along, target, filler):
+        n = lv.rows
+
+        def one_row(j, r):
+            conv_row(lv, w, target, j, r)
+
+        inner_rows(n, one_row)
+        end_rows(lv)
+        begin_tables(lv)
+        outer_rows(n, one_row)
+        end_tables(lv)
+        begin_strips(lv)
+        filler()
+        end_mirror(lv)
+        column_strips(lv, False)
+        end_strips(lv)
+        end_row(lv, one_row)
+        make_edges(lv, along)
+
+    level(lv1, w1, a1, body2, early_ocean)
+    fix(lv1, body2, (0, rows - 1))
     begin_rows(lv2)
-    exchange(lv2)
-    store_columns(lv2)
-    end_strips(lv2)
-    conv(lv2, w2, bodys)
+    fix(lv1, body2, range(1, rows - 1))
+    level(lv2, w2, a2, bodys, lambda: None)
+    fix(lv2, bodys, range(rows))
 
     def pool(i, carry):
         j, q = i // half_rows, i % half_rows
-        pair = bodys[j, pl.ds(pl.multiple_of((2 * q + 1) * C, C), 2 * C), pl.ds(0, side)]
+        pair = bodys[j, pl.ds(pl.multiple_of((2 * q + 1) * C, C), 2 * C), :]
         summed = jnp.dot(pair, down_mat[...], preferred_element_type=F32)
         at = pl.ds(pl.multiple_of((q + 1) * C, C), C)
-        body3[j, at, pl.ds(0, half_side)] = (summed[:C] + summed[C:]).astype(BF)
+        body3[j, at, :] = (summed[:C] + summed[C:]).astype(BF)
         return carry
 
     lax.fori_loop(0, faces * half_rows, pool, 0)
-
     begin_rows(lv3)
     begin_rows(lvs)
-    exchange(lv3)
-    store_columns(lv3)
-    end_strips(lv3)
-    conv(lv3, w3, body4)
-
+
+    def skip_tables():
+        end_rows(lvs)
+        begin_tables(lvs)
+
+    level(lv3, w3, a3, body4, skip_tables)
+    fix(lv3, body4, range(half_rows))
     begin_rows(lv4)
-    exchange(lvs)
-    store_columns(lvs)
-    exchange(lv4)
-    end_strips(lvs)
-
-    def store_coarse(j, total):
-        for k in range(rows + 2):
-            bodyc[j, pl.ds(k * C, C), pl.ds(side, 128)] = pltpu.roll(
-                total, (128 - 2 * ((k + 1) // 2)) % 128, 1
-            ).astype(BF)
-
-    def coarse_columns(j, carry):
-        column_strips(lv4, j, store_coarse)
-        return carry
-
-    end_mirror(lv4)
-    lax.fori_loop(0, faces, coarse_columns, 0)
-    end_strips(lv4)
-
-    def widen(j, carry):
-        for q in range(half_rows + 2):
+
+    def widen(j, qs):
+        for q in qs:
             made = jnp.dot(
                 body4[j, pl.ds(q * C, C), :], up_mat[...], preferred_element_type=F32
             ).astype(BF)
             for k in (2 * q - 1, 2 * q):
                 if 0 <= k <= rows + 1:
-                    bodyc[j, pl.ds(k * C, C), pl.ds(0, side)] = made
-        return carry
-
-    lax.fori_loop(0, faces, widen, 0)
-
-    def decode(i, carry):
-        j, r = i // rows, i % rows
+                    bodyc[j, pl.ds(k * C, C), :] = made
+
+    def widen_all(qs):
+        def body(j, carry):
+            widen(j, qs)
+            return carry
+
+        lax.fori_loop(0, faces, body, 0)
+
+    def tile_values(i, j, r, out, width, start):
+        where = pl.ds(start, width)
+        state = body1[j, pl.ds(pl.multiple_of(r * C + C, C), 16), where]
+        wet = jnp.broadcast_to(land_ref[j, pl.ds(r, 1), where] == 1, (8, width))
+        return (
+            state[:OUT_VARS].astype(F32) + out[:OUT_VARS],
+            jnp.where(wet, out[OUT_VARS:], 0.0),
+        )
+
+    def decode_row(j, r):
+        i = j * rows + r
         window = pl.ds(pl.multiple_of(r * C, C), 3 * C)
         product = jnp.dot(w4[...], bodys[j, window, :], preferred_element_type=F32)
         product += jnp.dot(w5[...], bodyc[j, window, :], preferred_element_type=F32)
-        decoded = jax.nn.gelu(taps(product, side)).astype(BF)
+        decoded = gelu(taps(product, side)).astype(BF)
         out = jnp.dot(head[...], decoded, preferred_element_type=F32)
-        state = body1[j, pl.ds(pl.multiple_of(r * C + C, C), 16), pl.ds(0, side)]
-        pred[i] = state[:OUT_VARS].astype(F32) + out[:OUT_VARS]
-        wet = jnp.broadcast_to(land_ref[j, pl.ds(r, 1), :] == 1, (8, side))
-        flux[i] = jnp.where(wet, out[OUT_VARS:], 0.0).astype(BF)
+        kept, wet = tile_values(i, j, r, out, side, 0)
+        pred[i] = kept
+        flux[i] = wet.astype(BF)
+
+    widen_all(range(1, half_rows + 1))
+    inner_rows(rows, decode_row)
+    end_tables(lvs)
+    begin_strips(lvs)
+    end_rows(lv4)
+    begin_tables(lv4)
+    widen_all((0, half_rows + 1))
+    outer_rows(rows, decode_row)
+    end_tables(lv4)
+    begin_strips(lv4)
+
+    def coarse_edges(j, carry):
+        extract(bodyc, edgec, side, j, range(rows + 2), True, True)
         return carry
 
-    lax.fori_loop(0, faces * rows, decode, 0)
+    lax.fori_loop(0, faces, coarse_edges, 0)
+    end_mirror(lvs)
+    column_strips(lvs, False)
+    end_strips(lvs)
+    end_mirror(lv4)
+    column_strips(lv4, True)
+    end_strips(lv4)
+    for cond, q, k, r in (
+        (is_top, 0, 0, 0),
+        (is_bot, half_rows + 1, rows + 1, rows - 1),
+    ):
+
+        @pl.when(cond)
+        def _(q=q, k=k, r=r):
+            def body(j, carry):
+                widen(j, (q,))
+                extract(bodys, lvs.edge, side, j, (k,), False, False)
+                extract(bodyc, edgec, side, j, (k,), False, False)
+                decode_row(j, r)
+                return carry
+
+            lax.fori_loop(0, faces, body, 0)
+
+    def decode_edges(j, carry):
+        terms = edge_terms(a4, lvs.edge[j], lvs.strip[j])
+        terms += edge_terms(a5, edgec[j], lv4.strip[j])
+        values = gelu(edge_sum(terms)).astype(BF)
+        out = jnp.dot(head[...], values, preferred_element_type=F32)
+        for r in range(rows):
+            low, high, is_low, is_high, left, right = patch(side, r, out)
+            i = j * rows + r
+            for part, mask, where in ((low, is_low[:8], left), (high, is_high[:8], right)):
+                kept, wet = tile_values(i, j, r, part, where.size, where.start)
+                pred[i, :, where] = jnp.where(mask, kept, pred[i, :, where])
+                old = flux[i, :, where].astype(F32)
+                flux[i, :, where] = jnp.where(mask, wet, old).astype(BF)
+        return carry
+
+    lax.fori_loop(0, faces, decode_edges, 0)
 
     flux_in = jnp.concatenate(
         [jnp.zeros((C, 2), F32), oin_ref[:, OCEAN_CH:], jnp.zeros((C, 2), F32)], axis=1
@@ -570,7 +727,7 @@
     def ocean(i, carry):
         slot = slot_ref[i]
         parts = jnp.dot(split, flux[i], preferred_element_type=F32)
-        hidden = jax.nn.gelu(
+        hidden = gelu(
             before[slot] + (parts[:C] + (parts[C : 2 * C] + parts[2 * C :]))
         )
         moved = jnp.sum(oout[...] * hidden, axis=0, keepdims=True)
@@ -639,12 +796,12 @@
     half_rows, half_side = rows // 2, side // 2
     vmem = pltpu.VMEM
     scratch = [
-        vmem((faces, (rows + 2) * C, side + 128), BF),
-        vmem((faces, (rows + 2) * C, side + 128), BF),
-        vmem((faces, (half_rows + 2) * C, half_side + 128), BF),
-        vmem((faces, (rows + 2) * C, side + 128), BF),
+        vmem((faces, (rows + 2) * C, side), BF),
+        vmem((faces, (rows + 2) * C, side), BF),
         vmem((faces, (half_rows + 2) * C, half_side), BF),
-        vmem((faces, (rows + 2) * C, side + 128), BF),
+        vmem((faces, (rows + 2) * C, side), BF),
+        vmem((faces, (half_rows + 2) * C, half_side), BF),
+        vmem((faces, (rows + 2) * C, side), BF),
         vmem((5, tiles * 16, side), BF),
         vmem((5, tiles * 16, half_side), BF),
         vmem((half_side, side), BF),
@@ -662,6 +819,13 @@
         vmem((slots, C, side), F32),
         vmem((slots, 1, side), F32),
         vmem((count, 1, side), F32),
+    ]
+    scratch += [vmem((3 * C, 3 * C), BF)] * 5
+    scratch += [
+        vmem((5, faces, C, 128), F32),
+        vmem((5, faces, C, 128), F32),
+        vmem((faces, C, 128), F32),
+        vmem((faces, C, 128), F32),
     ]
     for _ in range(5):
         scratch += [

time: 141 us -> 121 us (0.86)
  Pallas kernels: 133 us -> 112 us
    pallas_call x1, Pallas kernels: 133 us -> 112 us  [on_device(): pl.pallas_call(functools.partial(kernel, groups, tiles, rows, faces), out...]
where the time goes in v3:
time: 121 us; the launch traced here: 120 us
  Pallas kernels  112 us (93%)
  local copies, waits for them, and re-layouts  5.46 us (5%)
  other arithmetic  1.58 us (1%)
    pallas_call x1, Pallas kernels, on_device(): pl.pallas_call(functools.partial(kernel, groups, tiles, rows, faces), out...  112 us
    unnamed x14, local copies, waits for them, and re-layouts  3.77 us

profile of v3, /device:TPU:1, one launch (start us, length us, event | category | flops | bytes accessed | tf_op | source)
XLA Modules:
  0.0 119.9 jit_solution(8603504032449491081)
XLA Ops:
  0.6 0.0 copy-start.5
  0.6 0.6 copy-done.5
  1.3 0.2 convert_reduce_fusion
  1.5 0.0 copy-start.4
  1.5 0.6 copy-done.4
  2.1 0.1 select_reduce_fusion
  2.1 0.5 broadcast_add_fusion.inv_ref
  2.7 1.1 copy.20
  3.7 0.0 copy-start.3
  3.7 1.0 pad.4.clone
  4.7 0.0 copy-done.3
  4.7 0.7 copy.18.oin_ref
  5.4 0.0 copy-start
  5.4 112.2 %coupled_step.1 = (f32[24,8,256]{2,1,0:T(8,128)}, f32[64,1,256]{2,1,0:T(1,128)}) custom-call(s32[2,48]{1,0:T(2,128)} %bitcast.19, s32[64]{0:T(128)} %broadcast_add_fusion.inv_ref, s32[24]{0:T(128)} %copy-done.4, bf16[3,512,256]{2,1,0:T(8,128)(2,1)} %bitcast.13, s32[3,8,256]{2,1,0:T(8,128)} %land_ref.1, f32[64,2,256]{2,1,0:T(2,128)} %bitcast.16, ...), custom_call_target="tpu_custom_call" | custom-call | tf_op jit(solution)/shard_map/coupled_step/pallas_call | solution.py:844
  117.6 0.0 copy-start.2
  117.6 0.0 copy-done
  117.6 0.0 copy-start.1
  117.7 0.8 copy-done.2
  118.5 0.8 maximum_bitcast_fusion
  119.2 0.0 copy-done.1
  119.2 0.7 copy.22
  (3 shorter events, 0.1 us)
Async XLA Ops:
  0.6 0.7 copy-start.5
  1.5 0.6 copy-start.4
  3.7 1.0 copy-start.3
  5.4 112.2 %copy-start = (f32[1,1,64,2,256]{4,3,2,1,0:T(2,128)S(1)}, f32[1,1,64,2,256]{4,3,2,1,0:T(2,128)}, u32[]{:S(2)}) copy-start(f32[1,1,64,2,256]{4,3,2,1,0:T(2,128)} %param.16) | copy-start | bytes 393220
  117.6 0.8 copy-start.2
  117.6 1.6 %copy-start.1 = (f32[24,8,256]{2,1,0:T(8,128)S(1)}, f32[24,8,256]{2,1,0:T(8,128)}, u32[]{:S(2)}) copy-start(f32[24,8,256]{2,1,0:T(8,128)} %get-tuple-element.4) | copy-start | bytes 589828

commit v4 on v3

--- a/solution.py
+++ b/solution.py
@@ -54,15 +54,15 @@
     inv_ref,
     slot_ref,
     atmos_ref,
-    land_ref,
-    held_ref,
-    w1_ref,
-    w2_ref,
-    w3_ref,
-    w4_ref,
-    head_ref,
-    oin_ref,
-    oout_ref,
+    land_hbm,
+    held_hbm,
+    w1_hbm,
+    w2_hbm,
+    w3_hbm,
+    w4_hbm,
+    head_hbm,
+    oin_hbm,
+    oout_hbm,
     out_ref,
     sea_ref,
     body1,
@@ -76,7 +76,6 @@
     up_mat,
     down_mat,
     pred,
-    flux,
     visit,
     sea_out,
     sea_in,
@@ -99,6 +98,24 @@
     strips,
     edgec,
     made_edge,
+    skip_sum,
+    wet_edge,
+    before_edge,
+    state_edge,
+    out_vmem,
+    land_ref,
+    held_ref,
+    w1_ref,
+    w2_ref,
+    w3_ref,
+    w4_ref,
+    head_ref,
+    oin_ref,
+    oout_ref,
+    loaded,
+    oin_a,
+    oin_b,
+    split,
     *rest,
 ):
     bufs, (sems, misc) = rest[:-2], rest[-2:]
@@ -109,10 +126,28 @@
     is_top, is_bot = t == 0, t == tiles - 1
     last = tiles - 1
 
-    load = pltpu.make_async_copy(
-        atmos_ref, body1.at[:, pl.ds(C, rows * C), pl.ds(0, side)], misc.at[0]
+    inputs = (
+        (land_hbm, land_ref),
+        (held_hbm, held_ref),
+        (w1_hbm, w1_ref),
+        (w2_hbm, w2_ref),
+        (w3_hbm, w3_ref),
+        (w4_hbm, w4_ref),
+        (head_hbm, head_ref),
+        (oin_hbm, oin_ref),
+        (oout_hbm, oout_ref),
     )
-    load.start()
+    loads = [
+        pltpu.make_async_copy(src, dst, loaded.at[i]) for i, (src, dst) in enumerate(inputs)
+    ]
+    atmos_ch = atmos_ref.shape[2]
+    for j in range(faces):
+        for r in range(rows):
+            pltpu.make_async_copy(
+                atmos_ref.at[j, r], body1.at[j, pl.ds((r + 1) * C, atmos_ch)], misc.at[0]
+            ).start()
+    for load in loads:
+        load.start()
 
     levels = []
     for number, (n, s, body, sel) in enumerate(
@@ -159,6 +194,14 @@
     up_mat[...] = jnp.where(iota(shape, 1) // 2 == iota(shape, 0), 1.0, 0.0).astype(BF)
     shape = (side, half_side)
     down_mat[...] = jnp.where(iota(shape, 0) // 2 == iota(shape, 1), 0.25, 0.0).astype(BF)
+
+    for j in range(faces):
+        for r in range(rows):
+            spare = C - atmos_ch
+            if spare:
+                body1[j, pl.ds((r + 1) * C + atmos_ch, spare), :] = jnp.zeros((spare, side), BF)
+    for load in loads:
+        load.wait()
 
     for target, along, ref, first, width in (
         (w1, a1, w1_ref, 0, w1_ref.shape[2] // 3),
@@ -178,15 +221,30 @@
                 target[pl.ds(b * C, C), pl.ds(a * C, C)] = block.astype(BF)
                 along[pl.ds(a * C, C), pl.ds(b * C, C)] = block.astype(BF)
     made = head_ref[...].astype(F32)
-    gap = jnp.zeros((2, C), F32)
-    head[...] = jnp.concatenate([made[:OUT_VARS], gap, made[OUT_VARS:], gap], axis=0).astype(BF)
+    gap = jnp.zeros((FLUX_CH, C), F32)
+    head[...] = jnp.concatenate([made[:OUT_VARS]] + [made[OUT_VARS:]] * 3 + [gap], axis=0).astype(
+        BF
+    )
     diagonal = iota((C, C), 0) == iota((C, C), 1)
-    column = jnp.sum(
-        jnp.where(diagonal, jnp.broadcast_to(oout_ref[...], (C, C)), 0.0), axis=1, keepdims=True
-    )
-    oout[...] = jnp.broadcast_to(column, (C, side))
-
-    load.wait()
+
+    def column(row):
+        spread = jnp.where(diagonal, jnp.broadcast_to(row, (C, C)), 0.0)
+        return jnp.sum(spread, axis=1, keepdims=True)
+
+    oout[...] = jnp.broadcast_to(column(oout_ref[...]), oout.shape)
+    oin = [column(oin_ref[c : c + 1, :]) for c in range(OCEAN_CH + FLUX_CH)]
+    w_a, w_b = (jnp.broadcast_to(oin[c], (C, side)) for c in range(OCEAN_CH))
+    oin_a[...] = w_a
+    oin_b[...] = w_b
+    flux_in = jnp.concatenate(oin[OCEAN_CH:], axis=1)
+    first = flux_in.astype(BF)
+    second = (flux_in - first.astype(F32)).astype(BF)
+    third = (flux_in - first.astype(F32) - second.astype(F32)).astype(BF)
+    split[...] = jnp.concatenate(
+        [v.astype(F32) for v in (first, second, third)] + [jnp.zeros((C, FLUX_CH), F32)], axis=1
+    ).astype(BF)
+
+    drain(body1.at[:, pl.ds(0, rows * atmos_ch), :], misc.at[0])
     pl.semaphore_wait(barrier, tiles - 1 + groups - 1)
 
     def remote(src, dst, send, recv, device):
@@ -310,6 +368,13 @@
         edge[j] = total
         return total
 
+    def extract_inner(body, edge, n, s):
+        def one_face(j, carry):
+            extract(body, edge, s, j, range(1, n + 1), True, False)
+            return carry
+
+        lax.fori_loop(0, faces, one_face, 0)
+
     def begin_tables(lv):
         n, s = lv.rows, lv.side
         shape = (32, 128)
@@ -318,13 +383,13 @@
         pick = jnp.where((at == want) & (row % 16 < n + 2), 1.0, 0.0).astype(BF)
 
         def one_face(j, carry):
-            edge = extract(lv.body, lv.edge, s, j, range(n + 2), True, True)
+            edge = extract(lv.body, lv.edge, s, j, (0, n + 1), False, True)
             total = lax.dot_general(pick, edge.astype(BF), NT, preferred_element_type=F32)
             lv.tab[2 * j + 1] = jnp.concatenate([total[:16], total[16:]], axis=1).astype(BF)
             lv.tab[2 * j] = lv.scat_in[0, j] + lv.scat_in[1, j]
             return carry
 
-        lax.fori_loop(0, faces, one_face, 0)
+        lax.fori_loop(0, faces, one_face, 0, unroll=True)
         for d in range(1, groups):
             table_copy(lv, d).start()
         lv.tabs[pl.ds(f * 2 * faces, 2 * faces)] = lv.tab[...]
@@ -402,7 +467,7 @@
             lv.strip[j] = total
             return carry
 
-        lax.fori_loop(0, faces, one_face, 0)
+        lax.fori_loop(0, faces, one_face, 0, unroll=True)
 
     def end_mirror(lv):
         drain(lv.mirror, lv.sems.at[MIRROR_RECV])
@@ -425,7 +490,7 @@
             made_edge[j] = gelu(edge_sum(edge_terms(along, lv.edge[j], lv.strip[j])))
             return carry
 
-        lax.fori_loop(0, faces, one_face, 0)
+        lax.fori_loop(0, faces, one_face, 0, unroll=True)
 
     def patch(s, r, values):
         wide = min(s, 128)
@@ -448,7 +513,7 @@
                 target[j, here, right] = jnp.where(is_high, high, old).astype(BF)
             return carry
 
-        lax.fori_loop(0, faces, one_face, 0)
+        lax.fori_loop(0, faces, one_face, 0, unroll=True)
 
     def end_strips(lv):
         n, s = lv.rows, lv.side
@@ -498,12 +563,15 @@
         made = gelu(taps(product, s)).astype(BF)
         target[j, pl.ds(pl.multiple_of(r * C + C, C), C), :] = made
 
-    def inner_rows(n, one_row):
+    def inner_rows(first, stop, one_row):
+        count = stop - first
+
         def body(i, carry):
-            one_row(i // (n - 2), 1 + i % (n - 2))
-            return carry
-
-        lax.fori_loop(0, faces * (n - 2), body, 0)
+            one_row(i // count, first + i % count)
+            return carry
+
+        if count > 0:
+            lax.fori_loop(0, faces * count, body, 0)
 
     def outer_rows(n, one_row):
         def body(j, carry):
@@ -566,64 +634,116 @@
 
     def early_ocean():
         drain(visit.at[pl.ds(0, 2 * (tiles - 1))], misc.at[2])
-        w_a = jnp.broadcast_to(oin_ref[:, 0:1], (C, side))
-        w_b = jnp.broadcast_to(oin_ref[:, 1:2], (C, side))
 
         def one_slot(n, carry):
             old = visit[n]
-            total = w_a * old[:1] + w_b * old[1:]
+            total = oin_a[...] * old[:1] + oin_b[...] * old[1:]
             before[n] = total
-            moved = jnp.sum(oout[...] * gelu(total), axis=0, keepdims=True)
+            moved = jnp.sum(oout[:, :side] * gelu(total), axis=0, keepdims=True)
             idle[n] = old[:1] + moved
             return carry
 
-        lax.fori_loop(0, 2 * tiles, one_slot, 0)
-
-    def level(lv, w, along, target, filler):
+        lax.fori_loop(0, 2 * tiles, one_slot, 0, unroll=2)
+
+    def to_edges(total, row, r, wide):
+        spot = iota(total.shape, 1)
+        low, high = row[:, :wide], row[:, side - wide :]
+        if wide < 128:
+            zero = jnp.zeros((row.shape[0], 128 - wide), row.dtype)
+            low = jnp.concatenate([low, zero], axis=1)
+            high = jnp.concatenate([zero, high], axis=1)
+        total = jnp.where(spot == 2 * r, pltpu.roll(low, 2 * r, 1), total)
+        return jnp.where(spot == 65 + 2 * r, pltpu.roll(high, (66 + 2 * r) % 128, 1), total)
+
+    def ocean_edges():
+        wide = min(side, 128)
+
+        def one_face(j, carry):
+            wet = jnp.zeros((8, 128), F32)
+            state = jnp.zeros((8, 128), F32)
+            total = jnp.zeros((C, 128), F32)
+            for r in range(rows):
+                slot = slot_ref[j * rows + r]
+                land = jnp.broadcast_to(land_ref[j, pl.ds(r, 1), :], (8, side)).astype(F32)
+                wet = to_edges(wet, land, r, wide)
+                old = jnp.broadcast_to(visit[slot][:1], (8, side))
+                state = to_edges(state, old, r, wide)
+                total = to_edges(total, before[slot], r, wide)
+            wet_edge[j] = wet
+            state_edge[j] = state
+            before_edge[j] = total
+            return carry
+
+        lax.fori_loop(0, faces, one_face, 0)
+
+    def level(lv, w, along, target, held_back, fill_rows, fill_strips):
         n = lv.rows
 
         def one_row(j, r):
             conv_row(lv, w, target, j, r)
 
-        inner_rows(n, one_row)
+        extract_inner(lv.body, lv.edge, n, lv.side)
+        inner_rows(1, n - 1 - held_back, one_row)
+        fill_rows()
         end_rows(lv)
         begin_tables(lv)
         outer_rows(n, one_row)
         end_tables(lv)
         begin_strips(lv)
-        filler()
+        inner_rows(n - 1 - held_back, n - 1, one_row)
+        fill_strips()
         end_mirror(lv)
         column_strips(lv, False)
         end_strips(lv)
         end_row(lv, one_row)
         make_edges(lv, along)
 
-    level(lv1, w1, a1, body2, early_ocean)
+    def nothing():
+        pass
+
+    level(lv1, w1, a1, body2, 0, nothing, early_ocean)
     fix(lv1, body2, (0, rows - 1))
     begin_rows(lv2)
     fix(lv1, body2, range(1, rows - 1))
-    level(lv2, w2, a2, bodys, lambda: None)
-    fix(lv2, bodys, range(rows))
-
-    def pool(i, carry):
-        j, q = i // half_rows, i % half_rows
-        pair = bodys[j, pl.ds(pl.multiple_of((2 * q + 1) * C, C), 2 * C), :]
-        summed = jnp.dot(pair, down_mat[...], preferred_element_type=F32)
-        at = pl.ds(pl.multiple_of((q + 1) * C, C), C)
-        body3[j, at, :] = (summed[:C] + summed[C:]).astype(BF)
-        return carry
-
-    lax.fori_loop(0, faces * half_rows, pool, 0)
+    level(lv2, w2, a2, bodys, 2, nothing, ocean_edges)
+
+    def pool(qs):
+        def one_face(j, carry):
+            for q in qs:
+                pair = bodys[j, pl.ds((2 * q + 1) * C, 2 * C), :]
+                summed = jnp.dot(pair, down_mat[...], preferred_element_type=F32)
+                body3[j, pl.ds((q + 1) * C, C), :] = (summed[:C] + summed[C:]).astype(BF)
+            return carry
+
+        lax.fori_loop(0, faces, one_face, 0, unroll=True)
+
+    outer = (0, 1, rows - 2, rows - 1)
+    fix(lv2, bodys, outer)
+    pool((0, half_rows - 1))
     begin_rows(lv3)
+    fix(lv2, bodys, [r for r in range(rows) if r not in outer])
+    pool(range(1, half_rows - 1))
     begin_rows(lvs)
 
-    def skip_tables():
+    def skip_row(j, r):
+        window = pl.ds(pl.multiple_of(r * C, C), 3 * C)
+        product = jnp.dot(w4[...], bodys[j, window, :], preferred_element_type=F32)
+        skip_sum[j * rows + r] = taps(product, side)
+
+    def fill_rows3():
+        extract_inner(bodys, lvs.edge, rows, side)
+        inner_rows(1, rows // 2, skip_row)
+
+    def fill_strips3():
         end_rows(lvs)
         begin_tables(lvs)
-
-    level(lv3, w3, a3, body4, skip_tables)
-    fix(lv3, body4, range(half_rows))
+        outer_rows(rows, skip_row)
+        inner_rows(rows // 2, rows - 1, skip_row)
+
+    level(lv3, w3, a3, body4, 0, fill_rows3, fill_strips3)
+    fix(lv3, body4, (0, half_rows - 1))
     begin_rows(lv4)
+    fix(lv3, body4, range(1, half_rows - 1))
 
     def widen(j, qs):
         for q in qs:
@@ -639,32 +759,35 @@
             widen(j, qs)
             return carry
 
-        lax.fori_loop(0, faces, body, 0)
-
-    def tile_values(i, j, r, out, width, start):
+        lax.fori_loop(0, faces, body, 0, unroll=True)
+
+    def tile_values(j, r, out, width, start):
         where = pl.ds(start, width)
         state = body1[j, pl.ds(pl.multiple_of(r * C + C, C), 16), where]
-        wet = jnp.broadcast_to(land_ref[j, pl.ds(r, 1), where] == 1, (8, width))
+        wet = jnp.broadcast_to(land_ref[j, pl.ds(r, 1), where] == 1, (16, width))
         return (
             state[:OUT_VARS].astype(F32) + out[:OUT_VARS],
-            jnp.where(wet, out[OUT_VARS:], 0.0),
+            jnp.where(wet, out[OUT_VARS:], 0.0).astype(BF),
         )
 
     def decode_row(j, r):
         i = j * rows + r
         window = pl.ds(pl.multiple_of(r * C, C), 3 * C)
-        product = jnp.dot(w4[...], bodys[j, window, :], preferred_element_type=F32)
-        product += jnp.dot(w5[...], bodyc[j, window, :], preferred_element_type=F32)
-        decoded = gelu(taps(product, side)).astype(BF)
+        product = jnp.dot(w5[...], bodyc[j, window, :], preferred_element_type=F32)
+        decoded = gelu(skip_sum[i] + taps(product, side)).astype(BF)
         out = jnp.dot(head[...], decoded, preferred_element_type=F32)
-        kept, wet = tile_values(i, j, r, out, side, 0)
-        pred[i] = kept
-        flux[i] = wet.astype(BF)
+        pred[i], flux = tile_values(j, r, out, side, 0)
+        slot = slot_ref[i]
+        hidden = gelu(before[slot] + jnp.dot(split[...], flux, preferred_element_type=F32))
+        moved = jnp.sum(oout[:, :side] * hidden, axis=0, keepdims=True)
+        tile_sea[i] = visit[slot][:1] + moved
 
     widen_all(range(1, half_rows + 1))
-    inner_rows(rows, decode_row)
+    extract_inner(body4, lv4.edge, half_rows, half_side)
     end_tables(lvs)
     begin_strips(lvs)
+    early = 1 + (rows - 2) // 3
+    inner_rows(1, early, decode_row)
     end_rows(lv4)
     begin_tables(lv4)
     widen_all((0, half_rows + 1))
@@ -677,6 +800,7 @@
         return carry
 
     lax.fori_loop(0, faces, coarse_edges, 0)
+    inner_rows(early, rows - 1, decode_row)
     end_mirror(lvs)
     column_strips(lvs, False)
     end_strips(lvs)
@@ -694,6 +818,7 @@
                 widen(j, (q,))
                 extract(bodys, lvs.edge, side, j, (k,), False, False)
                 extract(bodyc, edgec, side, j, (k,), False, False)
+                skip_row(j, r)
                 decode_row(j, r)
                 return carry
 
@@ -704,37 +829,27 @@
         terms += edge_terms(a5, edgec[j], lv4.strip[j])
         values = gelu(edge_sum(terms)).astype(BF)
         out = jnp.dot(head[...], values, preferred_element_type=F32)
+        wet = jnp.concatenate([wet_edge[j]] * 2, axis=0) == 1.0
+        flux = jnp.where(wet, out[OUT_VARS:], 0.0).astype(BF)
+        hidden = gelu(before_edge[j] + jnp.dot(split[...], flux, preferred_element_type=F32))
+        moved = jnp.sum(oout[:, :128] * hidden, axis=0, keepdims=True)
+        sea = state_edge[j] + moved
         for r in range(rows):
             low, high, is_low, is_high, left, right = patch(side, r, out)
+            sea_low, sea_high, _, _, _, _ = patch(side, r, sea)
             i = j * rows + r
-            for part, mask, where in ((low, is_low[:8], left), (high, is_high[:8], right)):
-                kept, wet = tile_values(i, j, r, part, where.size, where.start)
+            for part, sea_part, mask, where in (
+                (low, sea_low, is_low[:8], left),
+                (high, sea_high, is_high[:8], right),
+            ):
+                kept, _ = tile_values(j, r, part, where.size, where.start)
                 pred[i, :, where] = jnp.where(mask, kept, pred[i, :, where])
-                old = flux[i, :, where].astype(F32)
-                flux[i, :, where] = jnp.where(mask, wet, old).astype(BF)
+                tile_sea[i, :, where] = jnp.where(
+                    mask[:1], sea_part[:1], tile_sea[i, :, where]
+                )
         return carry
 
-    lax.fori_loop(0, faces, decode_edges, 0)
-
-    flux_in = jnp.concatenate(
-        [jnp.zeros((C, 2), F32), oin_ref[:, OCEAN_CH:], jnp.zeros((C, 2), F32)], axis=1
-    )
-    first = flux_in.astype(BF)
-    second = (flux_in - first.astype(F32)).astype(BF)
-    third = (flux_in - first.astype(F32) - second.astype(F32)).astype(BF)
-    split = jnp.concatenate([first, second, third], axis=0)
-
-    def ocean(i, carry):
-        slot = slot_ref[i]
-        parts = jnp.dot(split, flux[i], preferred_element_type=F32)
-        hidden = gelu(
-            before[slot] + (parts[:C] + (parts[C : 2 * C] + parts[2 * C :]))
-        )
-        moved = jnp.sum(oout[...] * hidden, axis=0, keepdims=True)
-        tile_sea[i] = visit[slot][:1] + moved
-        return carry
-
-    lax.fori_loop(0, faces * rows, ocean, 0)
+    lax.fori_loop(0, faces, decode_edges, 0, unroll=True)
 
     def fill(n, carry):
         tile = inv_ref[n]
@@ -742,7 +857,7 @@
         sea_out[n] = jnp.where(used, tile_sea[jnp.where(used, tile, 0)], idle[n])
         return carry
 
-    lax.fori_loop(0, 2 * tiles, fill, 0)
+    lax.fori_loop(0, 2 * tiles, fill, 0, unroll=4)
     start_all(sea_copy)
     sea_in[pl.ds(2 * t, 2)] = sea_out[pl.ds(2 * t, 2)]
 
@@ -750,17 +865,22 @@
         sea = jnp.broadcast_to(tile_sea[i], (8, side))
         wet = jnp.broadcast_to(land_ref[i // rows, pl.ds(i % rows, 1), :] == 1, (8, side))
         wet = wet & (iota((8, side), 0) == 0)
-        out_ref[i] = jnp.where(wet, sea, pred[i])
+        out_vmem[i] = jnp.where(wet, sea, pred[i])
         return carry
 
     lax.fori_loop(0, faces * rows, surface, 0)
+    save = pltpu.make_async_copy(out_vmem, out_ref, loaded.at[0])
+    save.start()
     drain(sea_in.at[pl.ds(0, 2 * (tiles - 1))], misc.at[4])
-    sea_ref[...] = sea_in[...]
+    save_sea = pltpu.make_async_copy(sea_in, sea_ref, loaded.at[1])
+    save_sea.start()
 
     for lv in levels:
         finish_sends(lv)
     drain(held_ref.at[pl.ds(0, 2 * (tiles - 1))], misc.at[1])
     drain(sea_out.at[pl.ds(0, 2 * (tiles - 1))], misc.at[3])
+    save.wait()
+    save_sea.wait()
 
 
 def on_device(
@@ -781,8 +901,7 @@
     groups, tiles = lax.axis_size("face"), lax.axis_size("tile")
     count = faces * rows
     slots = ocean_state.shape[2]
-    atmos = jnp.pad(jnp.transpose(atmos_state, (1, 2, 0, 3)), ((0, 0), (0, 0), (0, C - channels), (0, 0)))
-    atmos = atmos.reshape(faces, rows * C, side)
+    atmos = jnp.transpose(atmos_state, (1, 2, 0, 3))
     owner_ids = owners[:, 0]
     same = owner_ids[:, None] == owner_ids[None, :]
     earlier = jnp.arange(count)[None, :] < jnp.arange(count)[:, None]
@@ -807,15 +926,14 @@
         vmem((half_side, side), BF),
         vmem((side, half_side), BF),
         vmem((count, OUT_VARS, side), F32),
-        vmem((count, 8, side), BF),
         vmem((slots, OCEAN_CH, side), F32),
         vmem((slots, 1, side), F32),
         vmem((slots, 1, side), F32),
     ]
     scratch += [vmem((3 * C, 3 * C), BF)] * 5
     scratch += [
-        vmem((16, C), BF),
-        vmem((C, side), F32),
+        vmem((24, C), BF),
+        vmem((C, max(side, 128)), F32),
         vmem((slots, C, side), F32),
         vmem((slots, 1, side), F32),
         vmem((count, 1, side), F32),
@@ -826,6 +944,29 @@
         vmem((5, faces, C, 128), F32),
         vmem((faces, C, 128), F32),
         vmem((faces, C, 128), F32),
+        vmem((count, C, side), F32),
+        vmem((faces, 8, 128), F32),
+        vmem((faces, C, 128), F32),
+        vmem((faces, 8, 128), F32),
+        vmem((count, OUT_VARS, side), F32),
+    ]
+    loaded = (
+        land_sea,
+        held,
+        conv_input,
+        conv_encode,
+        conv_coarse,
+        conv_decode,
+        output_head,
+        ocean_in.T,
+        ocean_out[None],
+    )
+    scratch += [vmem(v.shape, v.dtype) for v in loaded]
+    scratch += [
+        pltpu.SemaphoreType.DMA((len(loaded),)),
+        vmem((C, side), F32),
+        vmem((C, side), F32),
+        vmem((C, 16), BF),
     ]
     for _ in range(5):
         scratch += [
@@ -840,15 +981,15 @@
         ]
     scratch += [pltpu.SemaphoreType.DMA((5, SEM_COLS)), pltpu.SemaphoreType.DMA((5,))]
     smem = pl.BlockSpec(memory_space=pltpu.SMEM)
-    whole = pl.BlockSpec(memory_space=pltpu.VMEM)
+    anywhere = pl.BlockSpec(memory_space=pl.ANY)
     out, sea = pl.pallas_call(
         functools.partial(kernel, groups, tiles, rows, faces),
         out_shape=(
             jax.ShapeDtypeStruct((count, OUT_VARS, side), F32),
             jax.ShapeDtypeStruct((slots, 1, side), F32),
         ),
-        in_specs=[smem] * 3 + [pl.BlockSpec(memory_space=pl.ANY)] + [whole] * 9,
-        out_specs=(whole, whole),
+        in_specs=[smem] * 3 + [anywhere] * (1 + len(loaded)),
+        out_specs=(anywhere, anywhere),
         scratch_shapes=scratch,
         compiler_params=pltpu.CompilerParams(
             collective_id=0, has_side_effects=True, vmem_limit_bytes=56 * 1024 * 1024
@@ -859,15 +1000,7 @@
         inverse,
         slot,
         atmos,
-        land_sea,
-        held,
-        conv_input,
-        conv_encode,
-        conv_coarse,
-        conv_decode,
-        output_head,
-        ocean_in,
-        ocean_out[None],
+        *loaded,
     )
     atmos_next = jnp.transpose(out.reshape(faces, rows, OUT_VARS, side), (2, 0, 1, 3)).astype(BF)
     ocean_next = jnp.concatenate([sea, held[:, :1]], axis=1)

time: 121 us -> 108 us (0.89); the launches traced: 120 us -> 108 us
  Pallas kernels: 112 us -> 102 us
    pallas_call x1, Pallas kernels: 112 us -> 102 us  [on_device(): pl.pallas_call(functools.partial(kernel, groups, tiles, rows, faces), out...]
    unnamed x14 -> x11, local copies, waits for them, and re-layouts: 3.77 us -> 3.74 us
where the time goes in v4:
time: 108 us
  Pallas kernels  102 us (94%)
  local copies, waits for them, and re-layouts  4.45 us (4%)
  other arithmetic  1.58 us (1%)
    pallas_call x1, Pallas kernels, on_device(): pl.pallas_call(functools.partial(kernel, groups, tiles, rows, faces), out...  102 us
    unnamed x11, local copies, waits for them, and re-layouts  3.74 us

profile of v4, /device:TPU:1, one launch (start us, length us, event | category | flops | bytes accessed | tf_op | source)
XLA Modules:
  0.0 108.2 jit_solution(377687357689161711)
XLA Ops:
  0.6 0.0 copy-start.4
  0.6 0.6 copy-done.4
  1.3 0.2 convert_reduce_fusion
  1.5 0.0 copy-start.3
  1.5 0.5 copy-done.3
  2.0 0.1 select_reduce_fusion
  2.1 0.5 broadcast_add_fusion.inv_ref
  2.6 1.8 %copy.20 = bf16[32,3,8,256]{3,0,2,1:T(8,128)(2,1)} copy(bf16[32,3,8,256]{3,2,1,0:T(8,128)(2,1)} %param.12) | data formatting | bytes 786432 | tf_op args[0]
  4.4 0.0 copy-start
  4.4 101.5 %coupled_step.1 = (f32[24,8,256]{2,1,0:T(8,128)}, f32[64,1,256]{2,1,0:T(1,128)}) custom-call(s32[2,48]{1,0:T(2,128)} %bitcast.21, s32[64]{0:T(128)} %broadcast_add_fusion.inv_ref, s32[24]{0:T(128)} %copy-done.3, bf16[3,8,32,256]{3,2,1,0:T(8,128)(2,1)} %bitcast.15, s32[3,8,256]{2,1,0:T(8,128)} %land_hbm.1, f32[64,2,256]{2,1,0:T(2,128)} %bitcast.17, ...), custom_call_target="tpu_custom_call" | custom-call | tf_op jit(solution)/shard_map/coupled_step/pallas_call | solution.py:985
  105.9 0.0 copy-start.2
  105.9 0.0 copy-done
  105.9 0.0 copy-start.1
  106.0 0.8 copy-done.2
  106.8 0.8 maximum_bitcast_fusion
  107.5 0.0 copy-done.1
  107.6 0.7 copy.21
  (3 shorter events, 0.1 us)
Async XLA Ops:
  0.6 0.7 copy-start.4
  1.5 0.5 copy-start.3
  4.4 101.5 %copy-start = (f32[1,1,64,2,256]{4,3,2,1,0:T(2,128)S(1)}, f32[1,1,64,2,256]{4,3,2,1,0:T(2,128)}, u32[]{:S(2)}) copy-start(f32[1,1,64,2,256]{4,3,2,1,0:T(2,128)} %param.16) | copy-start | bytes 393220
  105.9 0.8 copy-start.2
  105.9 1.6 %copy-start.1 = (f32[24,8,256]{2,1,0:T(8,128)S(1)}, f32[24,8,256]{2,1,0:T(8,128)}, u32[]{:S(2)}) copy-start(f32[24,8,256]{2,1,0:T(8,128)} %get-tuple-element.4) | copy-start | bytes 589828

commit v5 on v4

--- a/solution.py
+++ b/solution.py
@@ -103,6 +103,7 @@
     before_edge,
     state_edge,
     out_vmem,
+    out_edge,
     land_ref,
     held_ref,
     w1_ref,
@@ -183,7 +184,10 @@
             q, x = iota(shape, 0), iota(shape, 1)
             k = q % 16
             start = (q // 16) * n
-            sel[0] = jnp.where((x == start + k - 1) & (k <= n + 1), 1.0, 0.0).astype(BF)
+            for at, low, high, base in ((0, 0, 10, 0), (5, 10, 15, 10), (6, 10, 15, 5)):
+                cell = k - base
+                inner = (k >= low) & (k < high) & (cell <= n + 1)
+                sel[at] = jnp.where((x == start + cell - 1) & inner, 1.0, 0.0).astype(BF)
             for at, least in ((1, 0), (2, 8)):
                 cell = start + k - least
                 inner = (k >= least) & (k < least + n)
@@ -301,15 +305,18 @@
 
             @pl.when(cond)
             def _(which=which):
-                for j in range(faces):
-                    start = C if which == 0 else n * C
-                    edge = lv.body[j, pl.ds(start, C), pl.ds(0, s)]
-                    zero = jnp.zeros_like(edge)
-                    both = jnp.concatenate([edge, zero] if which == 0 else [zero, edge], axis=0)
-                    piece = lax.dot_general(
-                        lv.sel[0], both, NT, preferred_element_type=F32
-                    ).astype(BF)
-                    lv.scat[:, j] = piece.reshape(tiles, 16, 2 * C)
+                start = C if which == 0 else n * C
+                a, b, c = (lv.body[j, pl.ds(start, C), pl.ds(0, s)] for j in range(faces))
+                zero = jnp.zeros_like(a)
+                total = jnp.zeros((tiles * 16, 2 * C), F32)
+                for at, pair in ((0, [a, b]), (5, [c, zero]), (6, [zero, c])):
+                    total += lax.dot_general(
+                        lv.sel[at],
+                        jnp.concatenate(pair, axis=0),
+                        NT,
+                        preferred_element_type=F32,
+                    )
+                lv.scat[...] = total.astype(BF).reshape(tiles, 16, 2 * C)
                 own = 0 if which == 0 else last
                 lv.scat_in[which] = lv.scat[own]
 
@@ -319,16 +326,23 @@
 
                 lax.fori_loop(1, tiles, send, 0)
 
-    def end_rows(lv):
+    def end_halos(lv):
         @pl.when(jnp.logical_not(is_top))
         def _():
             drain(lv.body.at[:, pl.ds(0, C), pl.ds(0, lv.side)], lv.sems.at[HALO_UP])
-            drain(lv.scat_in.at[0], lv.sems.at[SCAT_TOP])
 
         @pl.when(jnp.logical_not(is_bot))
         def _():
             n = lv.rows
             drain(lv.body.at[:, pl.ds((n + 1) * C, C), pl.ds(0, lv.side)], lv.sems.at[HALO_DOWN])
+
+    def end_scatter(lv):
+        @pl.when(jnp.logical_not(is_top))
+        def _():
+            drain(lv.scat_in.at[0], lv.sems.at[SCAT_TOP])
+
+        @pl.when(jnp.logical_not(is_bot))
+        def _():
             drain(lv.scat_in.at[1], lv.sems.at[SCAT_BOT])
 
     def table_copy(lv, d):
@@ -376,6 +390,7 @@
         lax.fori_loop(0, faces, one_face, 0)
 
     def begin_tables(lv):
+        end_halos(lv)
         n, s = lv.rows, lv.side
         shape = (32, 128)
         row, at = iota(shape, 0), iota(shape, 1)
@@ -386,10 +401,20 @@
             edge = extract(lv.body, lv.edge, s, j, (0, n + 1), False, True)
             total = lax.dot_general(pick, edge.astype(BF), NT, preferred_element_type=F32)
             lv.tab[2 * j + 1] = jnp.concatenate([total[:16], total[16:]], axis=1).astype(BF)
-            lv.tab[2 * j] = lv.scat_in[0, j] + lv.scat_in[1, j]
             return carry
 
         lax.fori_loop(0, faces, one_face, 0, unroll=True)
+        end_scatter(lv)
+        lows, highs = [], []
+        spot, row = iota((16, 128), 1), iota((16, 128), 0)
+        for which in range(2):
+            got = lv.scat_in[which].astype(F32)
+            swapped = pltpu.roll(got, 64, 1)
+            third = jnp.where(row < 5, pltpu.roll(got, 6, 0), pltpu.roll(swapped, 11, 0))
+            lows.append((got, swapped, third))
+            highs.append((swapped, got, pltpu.roll(third, 64, 1)))
+        for j in range(faces):
+            lv.tab[2 * j] = jnp.where(spot < 64, lows[0][j], highs[1][j]).astype(BF)
         for d in range(1, groups):
             table_copy(lv, d).start()
         lv.tabs[pl.ds(f * 2 * faces, 2 * faces)] = lv.tab[...]
@@ -571,21 +596,15 @@
             return carry
 
         if count > 0:
-            lax.fori_loop(0, faces * count, body, 0)
+            lax.fori_loop(0, faces * count, body, 0, unroll=3)
 
     def outer_rows(n, one_row):
-        def body(j, carry):
-            @pl.when(jnp.logical_not(is_top))
-            def _():
-                one_row(j, 0)
-
-            @pl.when(jnp.logical_not(is_bot))
-            def _():
-                one_row(j, n - 1)
-
-            return carry
-
-        lax.fori_loop(0, faces, body, 0)
+        for cond, r in ((is_top, 0), (is_bot, n - 1)):
+
+            @pl.when(jnp.logical_not(cond))
+            def _(r=r):
+                for j in range(faces):
+                    one_row(j, r)
 
     def end_row(lv, one_row):
         n = lv.rows
@@ -593,12 +612,9 @@
 
             @pl.when(cond)
             def _(k=k, r=r):
-                def body(j, carry):
+                for j in range(faces):
                     extract(lv.body, lv.edge, lv.side, j, (k,), False, False)
                     one_row(j, r)
-                    return carry
-
-                lax.fori_loop(0, faces, body, 0)
 
     def state_copy(d):
         dst = lax.rem(t + d, tiles)
@@ -685,7 +701,6 @@
         extract_inner(lv.body, lv.edge, n, lv.side)
         inner_rows(1, n - 1 - held_back, one_row)
         fill_rows()
-        end_rows(lv)
         begin_tables(lv)
         outer_rows(n, one_row)
         end_tables(lv)
@@ -730,15 +745,16 @@
         product = jnp.dot(w4[...], bodys[j, window, :], preferred_element_type=F32)
         skip_sum[j * rows + r] = taps(product, side)
 
+    skip_early = 1 + (rows - 2) // 3
+
     def fill_rows3():
         extract_inner(bodys, lvs.edge, rows, side)
-        inner_rows(1, rows // 2, skip_row)
+        inner_rows(1, skip_early, skip_row)
 
     def fill_strips3():
-        end_rows(lvs)
         begin_tables(lvs)
         outer_rows(rows, skip_row)
-        inner_rows(rows // 2, rows - 1, skip_row)
+        inner_rows(skip_early, rows - 1, skip_row)
 
     level(lv3, w3, a3, body4, 0, fill_rows3, fill_strips3)
     fix(lv3, body4, (0, half_rows - 1))
@@ -788,7 +804,6 @@
     begin_strips(lvs)
     early = 1 + (rows - 2) // 3
     inner_rows(1, early, decode_row)
-    end_rows(lv4)
     begin_tables(lv4)
     widen_all((0, half_rows + 1))
     outer_rows(rows, decode_row)
@@ -799,11 +814,19 @@
         extract(bodyc, edgec, side, j, range(rows + 2), True, True)
         return carry
 
-    lax.fori_loop(0, faces, coarse_edges, 0)
+    lax.fori_loop(0, faces, coarse_edges, 0, unroll=True)
     inner_rows(early, rows - 1, decode_row)
     end_mirror(lvs)
     column_strips(lvs, False)
     end_strips(lvs)
+    for cond, k, r in ((is_top, 0, 0), (is_bot, rows + 1, rows - 1)):
+
+        @pl.when(cond)
+        def _(k=k, r=r):
+            for j in range(faces):
+                extract(bodys, lvs.edge, side, j, (k,), False, False)
+                skip_row(j, r)
+
     end_mirror(lv4)
     column_strips(lv4, True)
     end_strips(lv4)
@@ -814,39 +837,38 @@
 
         @pl.when(cond)
         def _(q=q, k=k, r=r):
-            def body(j, carry):
+            for j in range(faces):
                 widen(j, (q,))
-                extract(bodys, lvs.edge, side, j, (k,), False, False)
                 extract(bodyc, edgec, side, j, (k,), False, False)
-                skip_row(j, r)
                 decode_row(j, r)
-                return carry
-
-            lax.fori_loop(0, faces, body, 0)
 
     def decode_edges(j, carry):
         terms = edge_terms(a4, lvs.edge[j], lvs.strip[j])
         terms += edge_terms(a5, edgec[j], lv4.strip[j])
         values = gelu(edge_sum(terms)).astype(BF)
         out = jnp.dot(head[...], values, preferred_element_type=F32)
+        out_edge[j] = out[:OUT_VARS]
         wet = jnp.concatenate([wet_edge[j]] * 2, axis=0) == 1.0
         flux = jnp.where(wet, out[OUT_VARS:], 0.0).astype(BF)
         hidden = gelu(before_edge[j] + jnp.dot(split[...], flux, preferred_element_type=F32))
         moved = jnp.sum(oout[:, :128] * hidden, axis=0, keepdims=True)
         sea = state_edge[j] + moved
         for r in range(rows):
+            low, high, is_low, is_high, left, right = patch(side, r, sea)
+            i = j * rows + r
+            for part, mask, where in ((low, is_low, left), (high, is_high, right)):
+                tile_sea[i, :, where] = jnp.where(mask[:1], part[:1], tile_sea[i, :, where])
+        return carry
+
+    def patch_edges(j, carry):
+        out = out_edge[j]
+        for r in range(rows):
             low, high, is_low, is_high, left, right = patch(side, r, out)
-            sea_low, sea_high, _, _, _, _ = patch(side, r, sea)
             i = j * rows + r
-            for part, sea_part, mask, where in (
-                (low, sea_low, is_low[:8], left),
-                (high, sea_high, is_high[:8], right),
-            ):
-                kept, _ = tile_values(j, r, part, where.size, where.start)
+            for part, mask, where in ((low, is_low, left), (high, is_high, right)):
+                state = body1[j, pl.ds((r + 1) * C, 16), where]
+                kept = state[:OUT_VARS].astype(F32) + part
                 pred[i, :, where] = jnp.where(mask, kept, pred[i, :, where])
-                tile_sea[i, :, where] = jnp.where(
-                    mask[:1], sea_part[:1], tile_sea[i, :, where]
-                )
         return carry
 
     lax.fori_loop(0, faces, decode_edges, 0, unroll=True)
@@ -857,9 +879,11 @@
         sea_out[n] = jnp.where(used, tile_sea[jnp.where(used, tile, 0)], idle[n])
         return carry
 
-    lax.fori_loop(0, 2 * tiles, fill, 0, unroll=4)
+    lax.fori_loop(0, 2 * tiles, fill, 0, unroll=8)
     start_all(sea_copy)
     sea_in[pl.ds(2 * t, 2)] = sea_out[pl.ds(2 * t, 2)]
+
+    lax.fori_loop(0, faces, patch_edges, 0, unroll=True)
 
     def surface(i, carry):
         sea = jnp.broadcast_to(tile_sea[i], (8, side))
@@ -868,7 +892,7 @@
         out_vmem[i] = jnp.where(wet, sea, pred[i])
         return carry
 
-    lax.fori_loop(0, faces * rows, surface, 0)
+    lax.fori_loop(0, faces * rows, surface, 0, unroll=4)
     save = pltpu.make_async_copy(out_vmem, out_ref, loaded.at[0])
     save.start()
     drain(sea_in.at[pl.ds(0, 2 * (tiles - 1))], misc.at[4])
@@ -921,8 +945,8 @@
         vmem((faces, (rows + 2) * C, side), BF),
         vmem((faces, (half_rows + 2) * C, half_side), BF),
         vmem((faces, (rows + 2) * C, side), BF),
-        vmem((5, tiles * 16, side), BF),
-        vmem((5, tiles * 16, half_side), BF),
+        vmem((7, tiles * 16, side), BF),
+        vmem((7, tiles * 16, half_side), BF),
         vmem((half_side, side), BF),
         vmem((side, half_side), BF),
         vmem((count, OUT_VARS, side), F32),
@@ -949,6 +973,7 @@
         vmem((faces, C, 128), F32),
         vmem((faces, 8, 128), F32),
         vmem((count, OUT_VARS, side), F32),
+        vmem((faces, OUT_VARS, 128), F32),
     ]
     loaded = (
         land_sea,
@@ -970,8 +995,8 @@
     ]
     for _ in range(5):
         scratch += [
-            vmem((tiles, faces, 16, 2 * C), BF),
-            vmem((2, faces, 16, 2 * C), BF),
+            vmem((tiles, 16, 2 * C), BF),
+            vmem((2, 16, 2 * C), BF),
             vmem((2 * faces, 16, 2 * C), BF),
             vmem((groups * 2 * faces, 16, 2 * C), BF),
             vmem((2, faces, 16, 2 * C), BF),

time: 108 us -> 95.7 us (0.89)
  Pallas kernels: 102 us -> 88.7 us
    pallas_call x1, Pallas kernels: 102 us -> 88.7 us  [on_device(): pl.pallas_call(functools.partial(kernel, groups, tiles, rows, faces), out...]
where the time goes in v5:
time: 95.7 us; the launch traced here: 95.5 us
  Pallas kernels  88.7 us (93%)
  local copies, waits for them, and re-layouts  4.45 us (5%)
  other arithmetic  1.58 us (2%)
    pallas_call x1, Pallas kernels, on_device(): pl.pallas_call(functools.partial(kernel, groups, tiles, rows, faces), out...  88.7 us
    unnamed x11, local copies, waits for them, and re-layouts  3.74 us

profile of v5, /device:TPU:1, one launch (start us, length us, event | category | flops | bytes accessed | tf_op | source)
XLA Modules:
  0.0 95.5 jit_solution(1256542606345358358)
XLA Ops:
  0.6 0.0 copy-start.4
  0.6 0.6 copy-done.4
  1.3 0.2 convert_reduce_fusion
  1.5 0.0 copy-start.3
  1.5 0.5 copy-done.3
  2.0 0.1 select_reduce_fusion
  2.1 0.5 broadcast_add_fusion.inv_ref
  2.6 1.8 %copy.20 = bf16[32,3,8,256]{3,0,2,1:T(8,128)(2,1)} copy(bf16[32,3,8,256]{3,2,1,0:T(8,128)(2,1)} %param.12) | data formatting | bytes 786432 | tf_op args[0]
  4.4 0.0 copy-start
  4.4 88.7 %coupled_step.1 = (f32[24,8,256]{2,1,0:T(8,128)}, f32[64,1,256]{2,1,0:T(1,128)}) custom-call(s32[2,48]{1,0:T(2,128)} %bitcast.21, s32[64]{0:T(128)} %broadcast_add_fusion.inv_ref, s32[24]{0:T(128)} %copy-done.3, bf16[3,8,32,256]{3,2,1,0:T(8,128)(2,1)} %bitcast.15, s32[3,8,256]{2,1,0:T(8,128)} %land_hbm.1, f32[64,2,256]{2,1,0:T(2,128)} %bitcast.17, ...), custom_call_target="tpu_custom_call" | custom-call | tf_op jit(solution)/shard_map/coupled_step/pallas_call | solution.py:1010
  93.2 0.0 copy-start.2
  93.2 0.0 copy-done
  93.2 0.0 copy-start.1
  93.3 0.8 copy-done.2
  94.0 0.8 maximum_bitcast_fusion
  94.8 0.0 copy-done.1
  94.8 0.7 copy.21
  (3 shorter events, 0.1 us)
Async XLA Ops:
  0.6 0.7 copy-start.4
  1.5 0.5 copy-start.3
  4.4 88.8 %copy-start = (f32[1,1,64,2,256]{4,3,2,1,0:T(2,128)S(1)}, f32[1,1,64,2,256]{4,3,2,1,0:T(2,128)}, u32[]{:S(2)}) copy-start(f32[1,1,64,2,256]{4,3,2,1,0:T(2,128)} %param.16) | copy-start | bytes 393220
  93.2 0.8 copy-start.2
  93.2 1.6 %copy-start.1 = (f32[24,8,256]{2,1,0:T(8,128)S(1)}, f32[24,8,256]{2,1,0:T(8,128)}, u32[]{:S(2)}) copy-start(f32[24,8,256]{2,1,0:T(8,128)} %get-tuple-element.4) | copy-start | bytes 589828

commit v6 on v5

--- a/solution.py
+++ b/solution.py
@@ -38,7 +38,7 @@
 
 class Level:
     def __init__(self, rows, side, body, sems, bufs, sel, edge, strip):
-        self.edge, self.strip = edge, strip
+        self.edge, self.strip, self.sent = edge, strip, C
         self.rows, self.side, self.body, self.sems = rows, side, body, sems
         self.scat, self.scat_in, self.tab, self.tabs, self.pick, self.gath = bufs[:6]
         self.send, self.mirror = bufs[6:]
@@ -200,10 +200,10 @@
     down_mat[...] = jnp.where(iota(shape, 0) // 2 == iota(shape, 1), 0.25, 0.0).astype(BF)
 
     for j in range(faces):
-        for r in range(rows):
+        for k in range(rows + 2):
             spare = C - atmos_ch
             if spare:
-                body1[j, pl.ds((r + 1) * C + atmos_ch, spare), :] = jnp.zeros((spare, side), BF)
+                body1[j, pl.ds(k * C + atmos_ch, spare), :] = jnp.zeros((spare, side), BF)
     for load in loads:
         load.wait()
 
@@ -264,8 +264,8 @@
     def halo_up(lv):
         n, s = lv.rows, lv.side
         return remote(
-            lv.body.at[:, pl.ds(C, C), pl.ds(0, s)],
-            lv.body.at[:, pl.ds((n + 1) * C, C), pl.ds(0, s)],
+            lv.body.at[:, pl.ds(C, lv.sent), pl.ds(0, s)],
+            lv.body.at[:, pl.ds((n + 1) * C, lv.sent), pl.ds(0, s)],
             lv.sems.at[HALO_SEND],
             lv.sems.at[HALO_DOWN],
             (f, jnp.maximum(t - 1, 0)),
@@ -274,8 +274,8 @@
     def halo_down(lv):
         n, s = lv.rows, lv.side
         return remote(
-            lv.body.at[:, pl.ds(n * C, C), pl.ds(0, s)],
-            lv.body.at[:, pl.ds(0, C), pl.ds(0, s)],
+            lv.body.at[:, pl.ds(n * C, lv.sent), pl.ds(0, s)],
+            lv.body.at[:, pl.ds(0, lv.sent), pl.ds(0, s)],
             lv.sems.at[HALO_DOWN_SEND],
             lv.sems.at[HALO_UP],
             (f, jnp.minimum(t + 1, last)),
@@ -292,14 +292,6 @@
 
     def begin_rows(lv):
         n, s = lv.rows, lv.side
-
-        @pl.when(jnp.logical_not(is_top))
-        def _():
-            halo_up(lv).start()
-
-        @pl.when(jnp.logical_not(is_bot))
-        def _():
-            halo_down(lv).start()
 
         for which, cond in ((0, is_top), (1, is_bot)):
 
@@ -326,15 +318,24 @@
 
                 lax.fori_loop(1, tiles, send, 0)
 
+        @pl.when(jnp.logical_not(is_top))
+        def _():
+            halo_up(lv).start()
+
+        @pl.when(jnp.logical_not(is_bot))
+        def _():
+            halo_down(lv).start()
+
     def end_halos(lv):
         @pl.when(jnp.logical_not(is_top))
         def _():
-            drain(lv.body.at[:, pl.ds(0, C), pl.ds(0, lv.side)], lv.sems.at[HALO_UP])
+            drain(lv.body.at[:, pl.ds(0, lv.sent), pl.ds(0, lv.side)], lv.sems.at[HALO_UP])
 
         @pl.when(jnp.logical_not(is_bot))
         def _():
             n = lv.rows
-            drain(lv.body.at[:, pl.ds((n + 1) * C, C), pl.ds(0, lv.side)], lv.sems.at[HALO_DOWN])
+            at = pl.ds((n + 1) * C, lv.sent)
+            drain(lv.body.at[:, at, pl.ds(0, lv.side)], lv.sems.at[HALO_DOWN])
 
     def end_scatter(lv):
         @pl.when(jnp.logical_not(is_top))
@@ -644,9 +645,12 @@
         lax.fori_loop(1, tiles, body, 0)
 
     lv1, lv2, lv3, lvs, lv4 = levels
+    lv1.sent = atmos_ch
     begin_rows(lv1)
-    start_all(state_copy)
-    visit[pl.ds(2 * t, 2)] = held_ref[pl.ds(2 * t, 2)]
+
+    def start_state():
+        start_all(state_copy)
+        visit[pl.ds(2 * t, 2)] = held_ref[pl.ds(2 * t, 2)]
 
     def early_ocean():
         drain(visit.at[pl.ds(0, 2 * (tiles - 1))], misc.at[2])
@@ -692,7 +696,7 @@
 
         lax.fori_loop(0, faces, one_face, 0)
 
-    def level(lv, w, along, target, held_back, fill_rows, fill_strips):
+    def level(lv, w, along, target, held_back, fill_rows, fill_tables, fill_strips):
         n = lv.rows
 
         def one_row(j, r):
@@ -702,6 +706,7 @@
         inner_rows(1, n - 1 - held_back, one_row)
         fill_rows()
         begin_tables(lv)
+        fill_tables()
         outer_rows(n, one_row)
         end_tables(lv)
         begin_strips(lv)
@@ -716,11 +721,16 @@
     def nothing():
         pass
 
-    level(lv1, w1, a1, body2, 0, nothing, early_ocean)
+    level(lv1, w1, a1, body2, min(rows - 2, 3), nothing, start_state, nothing)
     fix(lv1, body2, (0, rows - 1))
     begin_rows(lv2)
     fix(lv1, body2, range(1, rows - 1))
-    level(lv2, w2, a2, bodys, 2, nothing, ocean_edges)
+
+    def fill_strips2():
+        early_ocean()
+        ocean_edges()
+
+    level(lv2, w2, a2, bodys, 0, nothing, nothing, fill_strips2)
 
     def pool(qs):
         def one_face(j, carry):
@@ -738,7 +748,6 @@
     begin_rows(lv3)
     fix(lv2, bodys, [r for r in range(rows) if r not in outer])
     pool(range(1, half_rows - 1))
-    begin_rows(lvs)
 
     def skip_row(j, r):
         window = pl.ds(pl.multiple_of(r * C, C), 3 * C)
@@ -752,11 +761,14 @@
         inner_rows(1, skip_early, skip_row)
 
     def fill_strips3():
+        inner_rows(skip_early, rows - 1, skip_row)
         begin_tables(lvs)
         outer_rows(rows, skip_row)
-        inner_rows(skip_early, rows - 1, skip_row)
-
-    level(lv3, w3, a3, body4, 0, fill_rows3, fill_strips3)
+
+    def fill_tables3():
+        begin_rows(lvs)
+
+    level(lv3, w3, a3, body4, 0, fill_rows3, fill_tables3, fill_strips3)
     fix(lv3, body4, (0, half_rows - 1))
     begin_rows(lv4)
     fix(lv3, body4, range(1, half_rows - 1))
@@ -800,11 +812,11 @@
 
     widen_all(range(1, half_rows + 1))
     extract_inner(body4, lv4.edge, half_rows, half_side)
+    early = 1 + (rows - 2) // 2
+    inner_rows(1, early, decode_row)
+    begin_tables(lv4)
     end_tables(lvs)
     begin_strips(lvs)
-    early = 1 + (rows - 2) // 3
-    inner_rows(1, early, decode_row)
-    begin_tables(lv4)
     widen_all((0, half_rows + 1))
     outer_rows(rows, decode_row)
     end_tables(lv4)
@@ -889,7 +901,7 @@
         sea = jnp.broadcast_to(tile_sea[i], (8, side))
         wet = jnp.broadcast_to(land_ref[i // rows, pl.ds(i % rows, 1), :] == 1, (8, side))
         wet = wet & (iota((8, side), 0) == 0)
-        out_vmem[i] = jnp.where(wet, sea, pred[i])
+        out_vmem[i] = jnp.where(wet, sea, pred[i]).astype(BF)
         return carry
 
     lax.fori_loop(0, faces * rows, surface, 0, unroll=4)
@@ -972,7 +984,7 @@
         vmem((faces, 8, 128), F32),
         vmem((faces, C, 128), F32),
         vmem((faces, 8, 128), F32),
-        vmem((count, OUT_VARS, side), F32),
+        vmem((count, OUT_VARS, side), BF),
         vmem((faces, OUT_VARS, 128), F32),
     ]
     loaded = (
@@ -1010,7 +1022,7 @@
     out, sea = pl.pallas_call(
         functools.partial(kernel, groups, tiles, rows, faces),
         out_shape=(
-            jax.ShapeDtypeStruct((count, OUT_VARS, side), F32),
+            jax.ShapeDtypeStruct((count, OUT_VARS, side), BF),
             jax.ShapeDtypeStruct((slots, 1, side), F32),
         ),
         in_specs=[smem] * 3 + [anywhere] * (1 + len(loaded)),
@@ -1027,7 +1039,7 @@
         atmos,
         *loaded,
     )
-    atmos_next = jnp.transpose(out.reshape(faces, rows, OUT_VARS, side), (2, 0, 1, 3)).astype(BF)
+    atmos_next = jnp.transpose(out.reshape(faces, rows, OUT_VARS, side), (2, 0, 1, 3))
     ocean_next = jnp.concatenate([sea, held[:, :1]], axis=1)
     return atmos_next, ocean_next[None, None]
 

time: 95.7 us -> 94 us (0.982)
  Pallas kernels: 88.7 us -> 86.9 us
    pallas_call x1, Pallas kernels: 88.7 us -> 86.9 us  [on_device(): pl.pallas_call(functools.partial(kernel, groups, tiles, rows, faces), out...]
where the time goes in v6:
time: 94 us; the launch traced here: 93.8 us
  Pallas kernels  86.9 us (92%)
  local copies, waits for them, and re-layouts  4.58 us (5%)
  other arithmetic  1.57 us (2%)
    pallas_call x1, Pallas kernels, on_device(): pl.pallas_call(functools.partial(kernel, groups, tiles, rows, faces), out...  86.9 us
    unnamed x11, local copies, waits for them, and re-layouts  3.87 us

profile of v6, /device:TPU:1, one launch (start us, length us, event | category | flops | bytes accessed | tf_op | source)
XLA Modules:
  0.0 93.8 jit_solution(7052141315453369220)
XLA Ops:
  0.6 0.0 copy-start.4
  0.6 0.6 copy-done.4
  1.3 0.2 convert_reduce_fusion
  1.5 0.0 copy-start.3
  1.5 0.5 copy-done.3
  2.0 0.1 select_reduce_fusion
  2.1 0.5 broadcast_add_fusion.inv_ref
  2.6 1.8 %copy.20 = bf16[32,3,8,256]{3,0,2,1:T(8,128)(2,1)} copy(bf16[32,3,8,256]{3,2,1,0:T(8,128)(2,1)} %param.12) | data formatting | bytes 786432 | tf_op args[0]
  4.4 0.0 copy-start
  4.4 86.9 %coupled_step.1 = (bf16[24,8,256]{2,1,0:T(8,128)(2,1)}, f32[64,1,256]{2,1,0:T(1,128)}) custom-call(s32[2,48]{1,0:T(2,128)} %bitcast.21, s32[64]{0:T(128)} %broadcast_add_fusion.inv_ref, s32[24]{0:T(128)} %copy-done.3, bf16[3,8,32,256]{3,2,1,0:T(8,128)(2,1)} %bitcast.15, s32[3,8,256]{2,1,0:T(8,128)} %land_hbm.1, f32[64,2,256]{2,1,0:T(2,128)} %bitcast.16, ...), custom_call_target="tpu_custom_call" | custom-call | tf_op jit(solution)/shard_map/coupled_step/pallas_call | solution.py:1022
  91.3 0.0 copy-done
  91.4 0.0 copy-start.2
  91.4 0.8 copy-done.2
  92.2 0.0 copy-start.1
  92.2 0.8 maximum_bitcast_fusion
  93.0 0.1 copy-done.1
  93.1 0.7 copy.21
  (2 shorter events, 0.1 us)
Async XLA Ops:
  0.6 0.7 copy-start.4
  1.5 0.5 copy-start.3
  4.4 86.9 %copy-start = (f32[1,1,64,2,256]{4,3,2,1,0:T(2,128)S(1)}, f32[1,1,64,2,256]{4,3,2,1,0:T(2,128)}, u32[]{:S(2)}) copy-start(f32[1,1,64,2,256]{4,3,2,1,0:T(2,128)} %param.16) | copy-start | bytes 393220
  91.4 0.8 copy-start.2
  92.2 0.9 copy-start.1
